TPU v7x, 32 devices: a whole 2x2x4 slice. The times are simulated.
32 devices in a mesh: group: 2 (over core), replica: 16 (over z, y, x).
Axes of the slice: x: 2, y: 2, z: 4, core: 2. Of those that a mesh axis runs over, the one named last changes fastest.
Arguments:
- tokens: bfloat16 [32768, 1152], P(('group', 'replica')), may hold values from -6 to 6
- out_grad: bfloat16 [32768, 1152], P(('group', 'replica')), may hold values from -6 to 6
- ln1_gain: bfloat16 [1152], P('group'), may hold values from 0.5 to 1.5
- ln1_bias: bfloat16 [1152], P('group'), may hold values from -3 to 3
- q_weight: bfloat16 [1152, 1152], P('group'), may hold values from -0.1875 to 0.1875
- q_bias: bfloat16 [1152], P('group'), may hold values from -3 to 3
- k_weight: bfloat16 [1152, 1152], P('group'), may hold values from -0.1875 to 0.1875
- v_weight: bfloat16 [1152, 1152], P('group'), may hold values from -0.1875 to 0.1875
- v_bias: bfloat16 [1152], P('group'), may hold values from -3 to 3
- o_weight: bfloat16 [1152, 1152], P('group'), may hold values from -2 to 2
- o_bias: bfloat16 [1152], P('group'), may hold values from -3 to 3
- ln2_gain: bfloat16 [1152], P('group'), may hold values from 0.5 to 1.5
- ln2_bias: bfloat16 [1152], P('group'), may hold values from -3 to 3
- up_weight: bfloat16 [1152, 4304], P('group'), may hold values from -0.1875 to 0.1875
- up_bias: bfloat16 [4304], P('group'), may hold values from -3 to 3
- down_weight: bfloat16 [4304, 1152], P('group'), may hold values from -0.09375 to 0.09375
- down_bias: bfloat16 [1152], P('group'), may hold values from -3 to 3
Outputs:
- activations: bfloat16 [32768, 1152], P(('group', 'replica'))
- input_grad: bfloat16 [32768, 1152], P(('group', 'replica'))
- ln1_gain_grad: float32 [1152], P('group')
- ln1_bias_grad: float32 [1152], P('group')
- q_weight_grad: float32 [1152, 1152], P('group')
- q_bias_grad: float32 [1152], P('group')
- k_weight_grad: float32 [1152, 1152], P('group')
- v_weight_grad: float32 [1152, 1152], P('group')
- v_bias_grad: float32 [1152], P('group')
- o_weight_grad: float32 [1152, 1152], P('group')
- o_bias_grad: float32 [1152], P('group')
- ln2_gain_grad: float32 [1152], P('group')
- ln2_bias_grad: float32 [1152], P('group')
- up_weight_grad: float32 [1152, 4304], P('group')
- up_bias_grad: float32 [4304], P('group')
- down_weight_grad: float32 [4304, 1152], P('group')
- down_bias_grad: float32 [1152], P('group')
All inputs are finite; a program needn't handle non-finite values.
Results may differ from a plain program's by a relative error of at most 0.018.
Values may be sent and summed in bfloat16 or wider, within the bound.
A program may use at most 256 MiB of HBM per device.

v0:
```python
import jax
import jax.numpy as jnp
from jax import lax
from jax.sharding import PartitionSpec as P

HEADS = 16
PATCHES = 128


def layer_norm(values, gain, shift):
    center = values - jnp.mean(values, axis=-1, keepdims=True)
    spread = jnp.mean(center * center, axis=-1, keepdims=True)
    return center * lax.rsqrt(spread + 1e-06) * gain + shift


def gelu_tanh(values):
    return jax.nn.gelu(values, approximate=True)


def split_heads(rows):
    return rows.reshape(-1, PATCHES, HEADS, rows.shape[-1] // HEADS)


def head_logits(query, key_rows):
    factor = (query.shape[-1] // HEADS) ** (-0.5)
    query_h = split_heads(query)
    key_h = split_heads(key_rows)
    logits = (
        jnp.einsum("isha,itha->ihst", query_h, key_h, preferred_element_type=jnp.float32) * factor
    )
    return (logits, query_h, key_h, factor)


def attend(query, key_rows, value_rows):
    logits, query_h, key_h, factor = head_logits(query, key_rows)
    peak = jnp.max(logits, axis=-1, keepdims=True)
    log_total = peak + jnp.log(jnp.sum(jnp.exp(logits - peak), axis=-1, keepdims=True))
    weights_low = jnp.exp(logits - log_total).astype(jnp.bfloat16)
    mixed = jnp.einsum(
        "ihst,itha->isha", weights_low, split_heads(value_rows), preferred_element_type=jnp.float32
    )
    return (mixed.reshape(query.shape), log_total)


def attend_back(query, key_rows, value_rows, log_total, d_mixed):
    logits, query_h, key_h, factor = head_logits(query, key_rows)
    weights = jnp.exp(logits - log_total)
    weights_low = weights.astype(jnp.bfloat16)
    value_h = split_heads(value_rows)
    d_mix_h = split_heads(d_mixed)
    d_weights = jnp.einsum("isha,itha->ihst", d_mix_h, value_h, preferred_element_type=jnp.float32)
    d_logits = weights * (d_weights - jnp.sum(weights * d_weights, axis=-1, keepdims=True))
    d_low = d_logits.astype(jnp.bfloat16)
    d_query = (
        jnp.einsum("ihst,itha->isha", d_low, key_h, preferred_element_type=jnp.float32) * factor
    ).astype(jnp.bfloat16)
    d_key = (
        jnp.einsum("ihst,isha->itha", d_low, query_h, preferred_element_type=jnp.float32) * factor
    ).astype(jnp.bfloat16)
    d_value = jnp.einsum(
        "ihst,isha->itha", weights_low, d_mix_h, preferred_element_type=jnp.float32
    ).astype(jnp.bfloat16)
    return (d_query.reshape(query.shape), d_key.reshape(query.shape), d_value.reshape(query.shape))


def outer_rows(left, right):
    return jnp.einsum("ra,rb->ab", left, right, preferred_element_type=jnp.float32)


def back_rows(grads, weight):
    return jnp.einsum("rb,ab->ra", grads, weight, preferred_element_type=jnp.float32)


def column_sums(grads):
    return jnp.sum(grads.astype(jnp.float32), axis=0)


def shards(
    tokens,
    out_grad,
    ln1_gain,
    ln1_bias,
    q_weight,
    q_bias,
    k_weight,
    v_weight,
    v_bias,
    o_weight,
    o_bias,
    ln2_gain,
    ln2_bias,
    up_weight,
    up_bias,
    down_weight,
    down_bias,
):
    attn_full = (
        lax.all_gather(ln1_gain, "group", axis=0, tiled=True),
        lax.all_gather(ln1_bias, "group", axis=0, tiled=True),
        lax.all_gather(q_weight, "group", axis=0, tiled=True),
        lax.all_gather(q_bias, "group", axis=0, tiled=True),
        lax.all_gather(k_weight, "group", axis=0, tiled=True),
        lax.all_gather(v_weight, "group", axis=0, tiled=True),
        lax.all_gather(v_bias, "group", axis=0, tiled=True),
        lax.all_gather(o_weight, "group", axis=0, tiled=True),
        lax.all_gather(o_bias, "group", axis=0, tiled=True),
    )
    gain_one, shift_one, wq_full, bq_full, wk_full, wv_full, bv_full, wo_full, bo_full = attn_full
    input_f = tokens.astype(jnp.float32)
    gain_one_f = gain_one.astype(jnp.float32)
    shift_one_f = shift_one.astype(jnp.float32)
    normed1 = layer_norm(input_f, gain_one_f, shift_one_f).astype(jnp.bfloat16)
    query = (
        jnp.dot(normed1, wq_full, preferred_element_type=jnp.float32) + bq_full.astype(jnp.float32)
    ).astype(jnp.bfloat16)
    key_rows = jnp.dot(normed1, wk_full, preferred_element_type=jnp.float32).astype(jnp.bfloat16)
    value_rows = (
        jnp.dot(normed1, wv_full, preferred_element_type=jnp.float32) + bv_full.astype(jnp.float32)
    ).astype(jnp.bfloat16)
    mixed, log_total = attend(query, key_rows, value_rows)
    attn_in = mixed.astype(jnp.bfloat16)
    residual = (
        input_f
        + jnp.dot(attn_in, wo_full, preferred_element_type=jnp.float32)
        + bo_full.astype(jnp.float32)
    )
    mlp_full = (
        lax.all_gather(ln2_gain, "group", axis=0, tiled=True),
        lax.all_gather(ln2_bias, "group", axis=0, tiled=True),
        lax.all_gather(up_weight, "group", axis=0, tiled=True),
        lax.all_gather(up_bias, "group", axis=0, tiled=True),
        lax.all_gather(down_weight, "group", axis=0, tiled=True),
        lax.all_gather(down_bias, "group", axis=0, tiled=True),
    )
    gain_two, shift_two, wup_full, bup_full, wdown_full, bdown_full = mlp_full
    gain_two_f = gain_two.astype(jnp.float32)
    shift_two_f = shift_two.astype(jnp.float32)
    normed2 = layer_norm(residual, gain_two_f, shift_two_f).astype(jnp.bfloat16)
    pre_act = jnp.dot(normed2, wup_full, preferred_element_type=jnp.float32) + bup_full.astype(
        jnp.float32
    )
    hidden = gelu_tanh(pre_act).astype(jnp.bfloat16)
    output = (
        residual
        + jnp.dot(hidden, wdown_full, preferred_element_type=jnp.float32)
        + bdown_full.astype(jnp.float32)
    )
    mlp_back = (
        lax.all_gather(ln2_gain, "group", axis=0, tiled=True),
        lax.all_gather(ln2_bias, "group", axis=0, tiled=True),
        lax.all_gather(up_weight, "group", axis=0, tiled=True),
        lax.all_gather(up_bias, "group", axis=0, tiled=True),
        lax.all_gather(down_weight, "group", axis=0, tiled=True),
        lax.all_gather(down_bias, "group", axis=0, tiled=True),
    )
    wup_back = mlp_back[2]
    wdown_back = mlp_back[4]
    grad_out = out_grad.astype(jnp.float32)
    d_wdown = outer_rows(hidden, out_grad)
    d_bdown = column_sums(out_grad)
    d_hidden = back_rows(out_grad, wdown_back)
    unused_act, gelu_back = jax.vjp(gelu_tanh, pre_act)
    d_pre = gelu_back(d_hidden)[0].astype(jnp.bfloat16)
    d_wup = outer_rows(normed2, d_pre)
    d_bup = column_sums(d_pre)
    d_normed2 = back_rows(d_pre, wup_back)
    unused_two, norm_back_two = jax.vjp(layer_norm, residual, gain_two_f, shift_two_f)
    d_res_norm, d_gain_two, d_shift_two = norm_back_two(d_normed2)
    d_residual = grad_out + d_res_norm
    mlp_grads = (
        lax.psum_scatter(
            d_gain_two.astype(jnp.bfloat16), "group", scatter_dimension=0, tiled=True
        ).astype(jnp.float32),
        lax.psum_scatter(
            d_shift_two.astype(jnp.bfloat16), "group", scatter_dimension=0, tiled=True
        ).astype(jnp.float32),
        lax.psum_scatter(
            d_wup.astype(jnp.bfloat16), "group", scatter_dimension=0, tiled=True
        ).astype(jnp.float32),
        lax.psum_scatter(
            d_bup.astype(jnp.bfloat16), "group", scatter_dimension=0, tiled=True
        ).astype(jnp.float32),
        lax.psum_scatter(
            d_wdown.astype(jnp.bfloat16), "group", scatter_dimension=0, tiled=True
        ).astype(jnp.float32),
        lax.psum_scatter(
            d_bdown.astype(jnp.bfloat16), "group", scatter_dimension=0, tiled=True
        ).astype(jnp.float32),
    )
    attn_back = (
        lax.all_gather(ln1_gain, "group", axis=0, tiled=True),
        lax.all_gather(ln1_bias, "group", axis=0, tiled=True),
        lax.all_gather(q_weight, "group", axis=0, tiled=True),
        lax.all_gather(q_bias, "group", axis=0, tiled=True),
        lax.all_gather(k_weight, "group", axis=0, tiled=True),
        lax.all_gather(v_weight, "group", axis=0, tiled=True),
        lax.all_gather(v_bias, "group", axis=0, tiled=True),
        lax.all_gather(o_weight, "group", axis=0, tiled=True),
        lax.all_gather(o_bias, "group", axis=0, tiled=True),
    )
    wq_back = attn_back[2]
    wk_back = attn_back[4]
    wv_back = attn_back[5]
    wo_back = attn_back[7]
    d_attn = d_residual.astype(jnp.bfloat16)
    d_wout = outer_rows(attn_in, d_attn)
    d_bout = column_sums(d_attn)
    d_mixed = back_rows(d_attn, wo_back).astype(jnp.bfloat16)
    d_query, d_key, d_value = attend_back(query, key_rows, value_rows, log_total, d_mixed)
    d_wquery = outer_rows(normed1, d_query)
    d_bquery = column_sums(d_query)
    d_wkey = outer_rows(normed1, d_key)
    d_wvalue = outer_rows(normed1, d_value)
    d_bvalue = column_sums(d_value)
    d_normed1 = (
        back_rows(d_query, wq_back) + back_rows(d_key, wk_back) + back_rows(d_value, wv_back)
    )
    unused_one, norm_back_one = jax.vjp(layer_norm, input_f, gain_one_f, shift_one_f)
    d_in_norm, d_gain_one, d_shift_one = norm_back_one(d_normed1)
    d_input = (d_residual + d_in_norm).astype(jnp.bfloat16)
    attn_grads = (
        lax.psum_scatter(
            d_gain_one.astype(jnp.bfloat16), "group", scatter_dimension=0, tiled=True
        ).astype(jnp.float32),
        lax.psum_scatter(
            d_shift_one.astype(jnp.bfloat16), "group", scatter_dimension=0, tiled=True
        ).astype(jnp.float32),
        lax.psum_scatter(
            d_wquery.astype(jnp.bfloat16), "group", scatter_dimension=0, tiled=True
        ).astype(jnp.float32),
        lax.psum_scatter(
            d_bquery.astype(jnp.bfloat16), "group", scatter_dimension=0, tiled=True
        ).astype(jnp.float32),
        lax.psum_scatter(
            d_wkey.astype(jnp.bfloat16), "group", scatter_dimension=0, tiled=True
        ).astype(jnp.float32),
        lax.psum_scatter(
            d_wvalue.astype(jnp.bfloat16), "group", scatter_dimension=0, tiled=True
        ).astype(jnp.float32),
        lax.psum_scatter(
            d_bvalue.astype(jnp.bfloat16), "group", scatter_dimension=0, tiled=True
        ).astype(jnp.float32),
        lax.psum_scatter(
            d_wout.astype(jnp.bfloat16), "group", scatter_dimension=0, tiled=True
        ).astype(jnp.float32),
        lax.psum_scatter(
            d_bout.astype(jnp.bfloat16), "group", scatter_dimension=0, tiled=True
        ).astype(jnp.float32),
    )
    summed = (
        lax.psum(attn_grads[0].astype(jnp.bfloat16), "replica").astype(jnp.float32),
        lax.psum(attn_grads[1].astype(jnp.bfloat16), "replica").astype(jnp.float32),
        lax.psum(attn_grads[2].astype(jnp.bfloat16), "replica").astype(jnp.float32),
        lax.psum(attn_grads[3].astype(jnp.bfloat16), "replica").astype(jnp.float32),
        lax.psum(attn_grads[4].astype(jnp.bfloat16), "replica").astype(jnp.float32),
        lax.psum(attn_grads[5].astype(jnp.bfloat16), "replica").astype(jnp.float32),
        lax.psum(attn_grads[6].astype(jnp.bfloat16), "replica").astype(jnp.float32),
        lax.psum(attn_grads[7].astype(jnp.bfloat16), "replica").astype(jnp.float32),
        lax.psum(attn_grads[8].astype(jnp.bfloat16), "replica").astype(jnp.float32),
        lax.psum(mlp_grads[0].astype(jnp.bfloat16), "replica").astype(jnp.float32),
        lax.psum(mlp_grads[1].astype(jnp.bfloat16), "replica").astype(jnp.float32),
        lax.psum(mlp_grads[2].astype(jnp.bfloat16), "replica").astype(jnp.float32),
        lax.psum(mlp_grads[3].astype(jnp.bfloat16), "replica").astype(jnp.float32),
        lax.psum(mlp_grads[4].astype(jnp.bfloat16), "replica").astype(jnp.float32),
        lax.psum(mlp_grads[5].astype(jnp.bfloat16), "replica").astype(jnp.float32),
    )
    attn_grads = tuple(summed[:9])
    mlp_grads = tuple(summed[9:])
    return (output.astype(jnp.bfloat16), d_input) + tuple(attn_grads) + tuple(mlp_grads)


def solution(mesh):
    placed = (
        P(("group", "replica"), None),
        P(("group", "replica"), None),
        P("group"),
        P("group"),
        P("group", None),
        P("group"),
        P("group", None),
        P("group", None),
        P("group"),
        P("group", None),
        P("group"),
        P("group"),
        P("group"),
        P("group", None),
        P("group"),
        P("group", None),
        P("group"),
    )
    return jax.shard_map(
        shards,
        mesh=mesh,
        in_specs=placed,
        out_specs=(
            P(("group", "replica"), None),
            P(("group", "replica"), None),
            P("group"),
            P("group"),
            P("group", None),
            P("group"),
            P("group", None),
            P("group", None),
            P("group"),
            P("group", None),
            P("group"),
            P("group"),
            P("group"),
            P("group", None),
            P("group"),
            P("group", None),
            P("group"),
        ),
        check_vma=False,
    )
```

profile of v0, /device:TPU:0, one launch (start us, length us, event | category | flops | bytes accessed | tf_op | source)
XLA Modules:
  0.0 822.0 jit_solution(7776557863947844190)
XLA Ops:
  16.1 3.9 all-reduce.23
  20.9 2.8 all-gather.7.cloned.1.call-done
  23.7 6.8 add_convert_fusion.3
  30.5 9.6 %reshape.203 = bf16[8,128,16,72]{3,2,1,0:T(8,128)(2,1)} reshape(bf16[1024,1152]{1,0:T(8,128)(2,1)} %add_convert_fusion.3) | data formatting | bytes 4718592 | tf_op jit(solution)/shard_map/reshape | solution.py:21
  40.1 6.2 copy.71
  46.3 7.1 add_convert_fusion.2
  53.4 9.6 %reshape.204 = bf16[8,128,16,72]{3,2,1,0:T(8,128)(2,1)} reshape(bf16[1024,1152]{1,0:T(8,128)(2,1)} %add_convert_fusion.2) | data formatting | bytes 4718592 | tf_op jit(solution)/shard_map/reshape | solution.py:21
  63.0 6.2 copy.69
  69.2 6.9 convolution_convert_fusion.7
  76.0 9.7 %reshape.205 = bf16[8,128,16,72]{3,2,1,0:T(8,128)(2,1)} reshape(bf16[1024,1152]{1,0:T(8,128)(2,1)} %convolution_convert_fusion.7) | data formatting | bytes 4718592 | tf_op jit(solution)/shard_map/reshape | solution.py:21
  85.7 6.4 copy.70
  92.1 4.0 multiply_reduce_fusion.1
  96.1 2.4 exponential_reduce_fusion
  101.2 3.0 copy.73
  104.2 7.4 fusion.65
  114.3 25.8 %multiply_convert_fusion = (bf16[1024,4304]{0,1:T(8,128)(2,1)}, f32[1024,4304]{0,1:T(8,128)}) fusion(f32[4304]{0:T(1024)S(1)} %convert_element_type.232, bf16[1152,4304]{1,0:T(8,128)(2,1)} %all-gather.15.cloned.1.call-done, f32[1024,1152]{1,0:T(8,128)} %copy-done.3, f32[1152]{0:T(1024)S(1)} %convert_element_type.230, f32[1152]{0:T(1024)S(1)} %convert_element_type.229, ...), kind=kOutput, calls=%fused_computation.11 | convolution fusion | flops 10204381184 | bytes 41113408 | tf_op jit(solution)/shard_map/dot_general | solution.py:139
  140.1 32.2 %fusion.59 = (bf16[4304]{0:T(1024)(128)(2,1)}, bf16[1024,4304]{0,1:T(8,128)(2,1)}) fusion(f32[1024,4304]{0,1:T(8,128)} %get-tuple-element.72, f32[4304]{0:T(1024)S(1)} %convert_element_type.232, bf16[1024,1152]{1,0:T(8,128)(2,1)} %param.18, bf16[4304,1152]{1,0:T(8,128)(2,1)} %all-gather.17.cloned.1.call-done), kind=kOutput, calls=%fused_computation.95 | convolution fusion | flops 10251366400 | bytes 38745312 | tf_op jit(solution)/shard_map/rb,ab->ra/dot_general | solution.py:71
  172.3 21.2 %multiply_reduce_fusion.2 = (bf16[1152]{0:T(1024)(128)(2,1)}, f32[1024]{0:T(1024)S(1)}, bf16[1152]{0:T(1024)(128)(2,1)}, f32[1024,1152]{1,0:T(8,128)}) fusion(f32[1024,1152]{1,0:T(8,128)} %copy-done.3, f32[1024]{0:T(1024)S(1)} %fusion.47, f32[1024]{0:T(1024)S(1)} %broadcast_multiply_fusion, f32[1152]{0:T(1024)S(1)} %convert_element_type.229, ...), kind=kOutput, calls=%fused_computation.41 | convolution fusion | flops 10163844096 | bytes 28189696 | tf_op jit(solution)/shard_map/rb,ab->ra/dot_general | solution.py:71
  193.5 4.8 fusion.63
  202.2 4.8 convolution_convert_fusion.6
  207.0 9.6 %reshape.206 = bf16[8,128,16,72]{3,2,1,0:T(8,128)(2,1)} reshape(bf16[1024,1152]{1,0:T(8,128)(2,1)} %convolution_convert_fusion.6) | data formatting | bytes 4718592 | tf_op jit(solution)/shard_map/reshape | solution.py:21
  216.6 6.5 copy.75
  223.1 7.3 multiply_reduce_fusion
  230.5 5.1 multiply_convert_fusion.1
  240.4 5.2 convolution_convert_fusion.5
  245.9 5.9 fusion.25
  254.8 5.2 convolution_convert_fusion.4
  260.3 7.2 fusion.67
  270.5 5.2 convolution_convert_fusion.3
  275.8 7.1 convolution_convert_fusion.2
  283.4 19.1 %convolution_convert_fusion.1 = bf16[1152,4304]{1,0:T(8,128)(2,1)} fusion(bf16[1024,4304]{0,1:T(8,128)(2,1)} %get-tuple-element.58, f32[1024,1152]{1,0:T(8,128)} %copy-done.3, f32[1152]{0:T(1024)S(1)} %copy-done.33, f32[1152]{0:T(1024)S(1)} %convert_element_type.229, f32[1024]{0:T(1024)S(1)} %fusion.47, f32[1024]{0:T(1024)S(1)} %broadcast_multiply_fusion), kind=kOutput, calls=%fused_computation.3 | convolution fusion | flops 10165266432 | bytes 23467008 | tf_op jit(solution)/shard_map/ra,rb->ab/dot_general | solution.py:67
  302.5 17.9 %convolution_convert_fusion = bf16[4304,1152]{1,0:T(8,128)(2,1)} fusion(bf16[1024,4304]{0,1:T(8,128)(2,1)} %get-tuple-element.71, bf16[1024,1152]{1,0:T(8,128)(2,1)} %param.18), kind=kOutput, calls=%fused_computation.2 | convolution fusion | flops 10159368192 | bytes 21090304 | tf_op jit(solution)/shard_map/ra,rb->ab/dot_general | solution.py:67
  320.5 16.6 %fusion = bf16[2176,1152]{1,0:T(8,128)(2,1)} fusion(bf16[4304,1152]{1,0:T(8,128)(2,1)} %convolution_convert_fusion), kind=kCustom, calls=%all-reduce-scatter | all-reduce-scatter fusion | flops 5013505 | bytes 14930432
  337.9 2.1 collective-permute-start
  340.8 22.1 %concatenate = bf16[2200,1152]{1,0:T(8,128)(2,1)} concatenate(bf16[24,1152]{1,0:T(8,128)(2,1)S(1)} %collective-permute-done, bf16[2176,1152]{1,0:T(8,128)(2,1)} %fusion), dimensions={0} | concatenate | bytes 10137600
  363.0 5.0 constant_dynamic-slice_fusion
  370.0 6.2 fusion.32
  376.2 3.6 fusion.29
  379.9 4.5 fusion.58
  386.6 2.6 fusion.18
  389.2 3.7 all-reduce.22
  393.7 81.5 %all-reduce.20 = (bf16[576]{0:T(1024)(128)(2,1)S(1)}, bf16[576]{0:T(1024)(128)(2,1)S(1)}, bf16[576]{0:T(1024)(128)(2,1)S(1)}, bf16[576]{0:T(1024)(128)(2,1)S(1)}...) all-reduce(bf16[576]{0:T(1024)(128)(2,1)S(1)} %dynamic-slice.10, ...), channel_id=1, replica_groups=mesh['group'=2,'replica'=16] {'replica'}, use_global_device_ids=true, to_apply=%region_13.0 | all-reduce | flops 6760 | bytes 27040 | tf_op jit(solution)/shard_map/psum | solution.py:251
  480.5 6.8 add_convert_fusion
  487.4 18.4 %fusion.22 = bf16[1024,1152]{1,0:T(8,128)(2,1)} fusion(f32[1024,1152]{1,0:T(8,128)S(1)} %bitcast.84, bf16[1024,4304]{0,1:T(8,128)(2,1)} %get-tuple-element.71, bf16[4304,1152]{1,0:T(8,128)(2,1)} %all-gather.17.cloned.1.call-done, f32[1152]{0:T(1024)S(1)} %convert_element_type.234), kind=kOutput, calls=%fused_computation.54 | convolution fusion | flops 10157948928 | bytes 25813504 | tf_op jit(solution)/shard_map/dot_general | solution.py:145
  505.8 291.5 %all-reduce.26.cloned.1.call-done = (bf16[576,1152]{1,0:T(8,128)(2,1)}, bf16[576,1152]{1,0:T(8,128)(2,1)}, bf16[576,1152]{1,0:T(8,128)(2,1)}, bf16[576,1152]{1,0...) async-done(((bf16[576,1152]{1,0:T(8,128)(2,1)}, bf16[576,1152]{1,0:T(8,128)(2,1)}, bf16[576,1152]{1,0:T(8,128)(2,1)}, bf16[576,1152]{1,0:T(8,128)(2,1)}, ...) | async-done | bytes 15224848 | tf_op jit(solution)/shard_map/psum | solution.py:253
  797.3 3.2 convert_element_type.253
  805.7 4.7 convert_element_type.268
  810.4 4.5 convert_element_type.271
  (220 shorter events, 44.3 us)
Async XLA Ops:
  7.2 16.5 %all-gather.7.cloned.1.call-start = ((), (), s32[]{:S(2)}) async-start(), calls=%async_computation.5 | async-start | bytes 3981312 | tf_op jit(solution)/shard_map/all_gather | solution.py:103
  7.9 38.4 %all-gather.9.cloned.1.call-start = ((), (), s32[]{:S(2)}) async-start(), calls=%async_computation.6 | async-start | bytes 3981312 | tf_op jit(solution)/shard_map/all_gather | solution.py:100
  8.7 60.5 %all-gather.11.cloned.1.call-start = ((), (), s32[]{:S(2)}) async-start(), calls=%async_computation.7 | async-start | bytes 3981312 | tf_op jit(solution)/shard_map/all_gather | solution.py:102
  9.4 94.8 %all-gather.13.cloned.1.call-start = ((), (), s32[]{:S(2)}) async-start(), calls=%async_computation.8 | async-start | bytes 3981312 | tf_op jit(solution)/shard_map/all_gather | solution.py:105
  10.0 104.3 %all-gather.15.cloned.1.call-start = ((), (), s32[]{:S(2)}) async-start(), calls=%async_computation.9 | async-start | bytes 15040512 | tf_op jit(solution)/shard_map/all_gather | solution.py:130
  10.6 3.9 copy-start.42
  10.6 4.2 copy-start.43
  10.6 4.4 copy-start.44
  10.6 4.6 copy-start.45
  10.7 4.9 copy-start.46
  10.7 5.1 copy-start.36
  10.7 129.4 %all-gather.17.cloned.1.call-start = ((), (), s32[]{:S(2)}) async-start(), calls=%async_computation.10 | async-start | bytes 14874624 | tf_op jit(solution)/shard_map/all_gather | solution.py:132
  11.3 356.7 %reduce-scatter.8.cloned.1.call-start = ((), (), s32[]{:S(2)}) async-start(), calls=%async_computation.11 | async-start | bytes 3981312 | tf_op jit(solution)/shard_map/reduce_scatter | solution.py:228
  12.0 57.1 %copy-start.21 = (f32[1024]{0:T(1024)}, f32[1024]{0:T(1024)S(1)}, u32[]{:S(2)}) copy-start(f32[1024]{0:T(1024)S(1)} %broadcast_multiply_fusion.1) | copy-start | bytes 12292
  20.0 49.1 %copy-start.34 = (f32[1152]{0:T(1024)}, f32[1152]{0:T(1024)S(1)}, u32[]{:S(2)}) copy-start(f32[1152]{0:T(1024)S(1)} %convert_element_type.217) | copy-start | bytes 13828
  20.0 49.1 %copy-start.19 = (f32[1152]{0:T(1024)}, f32[1152]{0:T(1024)S(1)}, u32[]{:S(2)}) copy-start(f32[1152]{0:T(1024)S(1)} %convert_element_type.216) | copy-start | bytes 13828
  20.1 94.2 %copy-start.32 = (f32[1152]{0:T(1024)}, f32[1152]{0:T(1024)S(1)}, u32[]{:S(2)}) copy-start(f32[1152]{0:T(1024)S(1)} %convert_element_type.230) | copy-start | bytes 13828
  20.9 9.7 %copy-start.27 = (f32[1024]{0:T(1024)}, f32[1024]{0:T(1024)S(1)}, u32[]{:S(2)}) copy-start(f32[1024]{0:T(1024)S(1)} %fusion.19) | copy-start | bytes 12292
  20.9 48.3 %copy-start.25 = (f32[1024]{0:T(1024)}, f32[1024]{0:T(1024)S(1)}, u32[]{:S(2)}) copy-start(f32[1024]{0:T(1024)S(1)} %fusion.46) | copy-start | bytes 12292
  96.1 5.1 copy-start
  193.5 4.8 copy-start.8
  230.5 5.1 copy-start.6
  235.6 4.8 copy-start.20
  235.6 4.8 copy-start.22
  235.6 4.8 copy-start.26
  235.7 4.8 copy-start.35
  245.7 122.3 %reduce-scatter.10.cloned.1.call-start = ((), (), s32[]{:S(2)}) async-start(), calls=%async_computation.12 | async-start | bytes 3981312 | tf_op jit(solution)/shard_map/reduce_scatter | solution.py:234
  260.0 107.9 %reduce-scatter.12.cloned.1.call-start = ((), (), s32[]{:S(2)}) async-start(), calls=%async_computation.13 | async-start | bytes 3981312 | tf_op jit(solution)/shard_map/reduce_scatter | solution.py:237
  275.7 7.6 copy-start.33
  275.7 92.2 %reduce-scatter.14.cloned.1.call-start = ((), (), s32[]{:S(2)}) async-start(), calls=%async_computation.14 | async-start | bytes 3981312 | tf_op jit(solution)/shard_map/reduce_scatter | solution.py:243
  282.9 85.1 %reduce-scatter.16.cloned.1.call-start = ((), (), s32[]{:S(2)}) async-start(), calls=%async_computation.15 | async-start | bytes 15040512 | tf_op jit(solution)/shard_map/reduce_scatter | solution.py:177
  302.5 494.8 %all-reduce.26.cloned.1.call-start = ((), (), s32[]{:S(2)}) async-start(), calls=%async_computation.16 | async-start | bytes 30560256 | tf_op jit(solution)/shard_map/psum | solution.py:253
  337.9 3.0 collective-permute-start
  370.0 6.2 copy-start.13
  370.0 6.2 copy-start.49
  379.8 4.6 copy-start.28
  384.4 4.8 copy-start.29
  384.4 4.8 copy-start.30
  384.4 4.8 copy-start.31
  384.4 4.8 copy-start.38
  384.4 4.8 copy-start.39
  384.5 96.1 %copy-start.24 = (f32[1024]{0:T(1024)S(1)}, f32[1024]{0:T(1024)}, u32[]{:S(2)}) copy-start(f32[1024]{0:T(1024)} %copy-done.23) | copy-start | bytes 12292
  386.6 100.8 %slice-start = ((s8[4718592]{0:T(1024)(128)(4,1)}), s8[524288]{0:T(1024)(128)(4,1)S(1)}, s32[]{:S(2)}) async-start(s8[4718592]{0:T(1024)(128)(4,1)} %bitcast.83), calls=%async_computation.17 | async-start | bytes 1048576
  480.5 6.8 slice-start.1
  797.3 4.9 copy-start.17
  800.4 5.1 slice-start.2
  803.8 6.6 slice-start.4
  805.7 4.7 slice-start.5
  (21 other events, 54.5 us)
Sparse Core Ops, SparseCore 0:
  9.6 14.0 all-gather.6
  25.2 12.5 all-gather.8
  39.4 12.5 all-gather.10
  53.4 12.5 all-gather.12
  67.4 23.5 all-gather.14
  92.4 23.4 all-gather.16
  245.8 11.4 reduce-scatter.7
  260.1 11.4 reduce-scatter.9
  275.8 11.4 reduce-scatter.11
  290.0 11.4 reduce-scatter.13
  304.3 19.7 reduce-scatter.15
  368.1 429.0 all-reduce.25
where the time goes:
time: 827 us; the launch traced here: 822 us
  waiting for transfers between devices  298 us (36%)
  matrix products  233 us (28%)
  local copies, waits for them, and re-layouts  115 us (14%)
  blocking collectives  106 us (13%)
  other arithmetic  48.1 us (6%)
  between operations  18.6 us (2%)
    psum x1, waiting for transfers between devices, shards(): lax.psum(attn_grads[2].astype(jnp.bfloat16), 'replica').astype(jnp.float32)  291 us
    psum x1, blocking collectives, shards(): lax.psum(attn_grads[0].astype(jnp.bfloat16), 'replica').astype(jnp.float32)  81.5 us
    dot_general x6, matrix products, back_rows(): jnp.einsum('rb,ab->ra', grads, weight, preferred_element_type=jnp.float32)  72.5 us
    reshape x8, local copies, waits for them, and re-layouts, split_heads(): return rows.reshape(-1, PATCHES, HEADS, rows.shape[-1] // HEADS)  63.6 us
    dot_general x6, matrix products, outer_rows(): jnp.einsum('ra,rb->ab', left, right, preferred_element_type=jnp.float32)  59.8 us
    unnamed x143, local copies, waits for them, and re-layouts  43.9 us
    dot_general x1, matrix products, shards(): jnp.dot(normed2, wup_full, preferred_element_type=jnp.float32)  25.8 us
    unnamed x3, blocking collectives  24.3 us
  transfers between devices with their start and end apart: 13, of which 3 were waited for; matrix products, arithmetic and copies ran while one was open for 34% of the time, Pallas kernels for 0%

commit v1 on v0

--- a/solution.py
+++ b/solution.py
@@ -1,6 +1,10 @@
+import functools
+
 import jax
 import jax.numpy as jnp
 from jax import lax
+from jax.experimental import pallas as pl
+from jax.experimental.pallas import tpu as pltpu
 from jax.sharding import PartitionSpec as P
 
 HEADS = 16
@@ -269,6 +273,728 @@
     return (output.astype(jnp.bfloat16), d_input) + tuple(attn_grads) + tuple(mlp_grads)
 
 
+MESH = pl.DeviceIdType.MESH
+bf16 = jnp.bfloat16
+f32 = jnp.float32
+ANY = pl.BlockSpec(memory_space=pl.ANY)
+WIDTH = 1152
+HALF = 576
+FF = 4304
+FF_HALF = 2152
+TILES = 17
+TILE = 128
+FF_PAD = 2 * TILES * TILE
+FIRST = 320
+SECOND = 256
+
+
+class Place:
+    def __init__(self):
+        self.core = lax.axis_index("group")
+        chip = lax.axis_index("replica")
+        self.chip = chip
+        self.x = lax.rem(chip, 2)
+        self.y = lax.rem(chip // 2, 2)
+        self.z = chip // 4
+        self.x_pair = chip + 1 - 2 * self.x
+        self.y_pair = chip + 2 - 4 * self.y
+        self.z_pair = chip + 4 - 8 * lax.rem(self.z, 2)
+        self.inner = (self.z == 1) | (self.z == 2)
+        self.outer = jnp.logical_not(self.inner)
+        self.mid_pair = jnp.where(self.inner, chip + 12 - 8 * self.z, chip)
+        self.z_half = lax.rem(self.z // 2, 2)
+
+    def barrier(self):
+        sem = pltpu.get_barrier_semaphore()
+
+        def greet(core, chip):
+            pl.semaphore_signal(sem, inc=1, device_id=(core, chip), device_id_type=MESH)
+
+        greet(1 - self.core, self.chip)
+        greet(self.core, self.x_pair)
+        greet(self.core, self.y_pair)
+        greet(self.core, self.z_pair)
+
+        @pl.when(self.inner)
+        def _():
+            greet(self.core, self.mid_pair)
+            pl.semaphore_wait(sem, 5)
+
+        @pl.when(self.outer)
+        def _():
+            pl.semaphore_wait(sem, 4)
+
+    def copy(self, source, target, sent, got, chip):
+        return pltpu.make_async_remote_copy(
+            source, target, sent, got, device_id=(self.core, chip), device_id_type=MESH
+        )
+
+    def copy_sibling(self, source, target, sent, got):
+        return pltpu.make_async_remote_copy(
+            source, target, sent, got, device_id=(1 - self.core, self.chip), device_id_type=MESH
+        )
+
+
+def aligned(value, unit):
+    return pl.multiple_of(value, unit)
+
+
+def add_rows(total, landed, chunk, start, count):
+    rows = pl.ds(start, count)
+    total[chunk, rows, :] = (
+        total[chunk, rows, :].astype(f32) + landed.astype(f32)
+    ).astype(bf16)
+
+
+class TreeFirst:
+    steps = 9
+
+    def __init__(self, place, total, final, landing, sent, got, kept):
+        self.at = place
+        self.total = total
+        self.final = final
+        self.kept = kept
+        self.land = landing
+        self.sent = sent
+        self.got = got
+        n = total.shape[1]
+        self.n = n
+        p = place
+        self.own = [
+            (0, n),
+            (aligned(p.z_half * (n // 2), n // 2), n // 2),
+        ]
+        self.other = [None, (aligned((1 - p.z_half) * (n // 2), n // 2), n // 2)]
+        for bit, part in ((p.y, n // 4), (p.x, n // 8)):
+            base = self.own[-1][0]
+            self.own.append((aligned(base + bit * part, part), part))
+            self.other.append((aligned(base + (1 - bit) * part, part), part))
+        self.peer = [p.z_pair, p.mid_pair, p.y_pair, p.x_pair]
+
+    def rows(self, chunk, span):
+        return self.total.at[chunk, pl.ds(span[0], span[1]), :]
+
+    def ends(self, chunk, span):
+        return self.final.at[chunk, pl.ds(span[0], span[1]), :]
+
+    def send(self, k, chunk):
+        sent, got = self.sent.at[k, chunk], self.got.at[k, chunk]
+        if k < 4:
+            span = self.own[0] if k == 0 else self.other[k]
+            return self.at.copy(
+                self.rows(chunk, span), self.land[k].at[chunk], sent, got, self.peer[k]
+            )
+        level = 7 - k
+        target = self.ends(chunk, self.own[level])
+        source = self.rows(chunk, self.own[3]) if k == 4 else target
+        return self.at.copy(source, target, sent, got, self.peer[level])
+
+    def keep(self, chunk):
+        return pltpu.make_async_copy(
+            self.rows(chunk, self.own[3]), self.ends(chunk, self.own[3]), self.kept.at[chunk]
+        )
+
+    def arrive(self, k, chunk):
+        if k < 4:
+            landed = self.land[k].at[chunk]
+        else:
+            level = 7 - k
+            landed = self.ends(chunk, self.own[0] if level == 0 else self.other[level])
+        self.at.copy(
+            landed, landed, self.sent.at[k, chunk], self.got.at[k, chunk], self.at.z_pair
+        ).wait_recv()
+
+    def step(self, k, chunk):
+        at = self.at
+        if k == 0:
+
+            @pl.when(at.outer)
+            def _():
+                self.send(0, chunk).start()
+
+        elif k <= 7:
+
+            @pl.when(at.inner)
+            def _():
+                self.arrive(k - 1, chunk)
+                if k <= 4:
+                    add_rows(self.total, self.land[k - 1][chunk], chunk, *self.own[k - 1])
+                if k == 4:
+                    self.keep(chunk).start()
+                if k == 5:
+                    self.keep(chunk).wait()
+                self.send(k, chunk).start()
+
+        else:
+
+            @pl.when(at.inner)
+            def _():
+                for j in range(1, 8):
+                    self.send(j, chunk).wait_send()
+
+            @pl.when(at.outer)
+            def _():
+                self.arrive(7, chunk)
+                self.send(0, chunk).wait_send()
+
+
+class PlaneFirst:
+    steps = 8
+
+    def __init__(self, place, total, final, base, n, x_first, landing, sent, got, kept):
+        self.at = place
+        self.total = total
+        self.final = final
+        self.kept = kept
+        self.land = landing
+        self.sent = sent
+        self.got = got
+        p = place
+        if x_first:
+            one, two = (p.x, p.x_pair), (p.y, p.y_pair)
+        else:
+            one, two = (p.y, p.y_pair), (p.x, p.x_pair)
+        self.peer_one, self.peer_two = one[1], two[1]
+        start = aligned(base + one[0] * (n // 2), 16)
+        self.half = (start, n // 2)
+        self.half_other = (aligned(base + (1 - one[0]) * (n // 2), 16), n // 2)
+        self.quarter = (aligned(start + two[0] * (n // 4), 16), n // 4)
+        self.quarter_other = (aligned(start + (1 - two[0]) * (n // 4), 16), n // 4)
+
+    def rows(self, chunk, span):
+        return self.total.at[chunk, pl.ds(span[0], span[1]), :]
+
+    def ends(self, chunk, span):
+        return self.final.at[chunk, pl.ds(span[0], span[1]), :]
+
+    def keep(self, chunk):
+        return pltpu.make_async_copy(
+            self.rows(chunk, self.quarter), self.ends(chunk, self.quarter), self.kept.at[chunk]
+        )
+
+    def send(self, k, chunk):
+        at = self.at
+        quarter = self.rows(chunk, self.quarter)
+        quarter_end = self.ends(chunk, self.quarter)
+        half_end = self.ends(chunk, self.half)
+        source, target, peer = (
+            (self.rows(chunk, self.half_other), self.land[0].at[chunk], self.peer_one),
+            (self.rows(chunk, self.quarter_other), self.land[1].at[chunk], self.peer_two),
+            (quarter, self.land[2].at[chunk], at.z_pair),
+            (quarter, self.land[3].at[chunk], at.mid_pair),
+            (quarter, quarter_end, at.z_pair),
+            (quarter_end, quarter_end, self.peer_two),
+            (half_end, half_end, self.peer_one),
+        )[k]
+        return at.copy(source, target, self.sent.at[k, chunk], self.got.at[k, chunk], peer)
+
+    def arrive(self, k, chunk):
+        if k < 4:
+            landed = self.land[k].at[chunk]
+        else:
+            landed = self.ends(
+                chunk, (self.quarter, self.quarter_other, self.half_other)[k - 4]
+            )
+        self.at.copy(
+            landed, landed, self.sent.at[k, chunk], self.got.at[k, chunk], self.at.z_pair
+        ).wait_recv()
+
+    def step(self, k, chunk):
+        at = self.at
+        if k == 0:
+            self.send(0, chunk).start()
+        elif k == 1:
+            self.arrive(0, chunk)
+            add_rows(self.total, self.land[0][chunk], chunk, *self.half)
+            self.send(1, chunk).start()
+        elif k == 2:
+            self.arrive(1, chunk)
+            add_rows(self.total, self.land[1][chunk], chunk, *self.quarter)
+
+            @pl.when(at.outer)
+            def _():
+                self.send(2, chunk).start()
+
+        elif k == 3:
+
+            @pl.when(at.inner)
+            def _():
+                self.arrive(2, chunk)
+                add_rows(self.total, self.land[2][chunk], chunk, *self.quarter)
+                self.send(3, chunk).start()
+
+        elif k == 4:
+
+            @pl.when(at.inner)
+            def _():
+                self.arrive(3, chunk)
+                self.send(3, chunk).wait_send()
+                add_rows(self.total, self.land[3][chunk], chunk, *self.quarter)
+                self.send(4, chunk).start()
+                self.keep(chunk).start()
+
+        elif k == 5:
+
+            @pl.when(at.inner)
+            def _():
+                self.keep(chunk).wait()
+
+            @pl.when(at.outer)
+            def _():
+                self.arrive(4, chunk)
+
+            self.send(5, chunk).start()
+        elif k == 6:
+            self.arrive(5, chunk)
+            self.send(6, chunk).start()
+        else:
+            self.arrive(6, chunk)
+            for j in (0, 1, 5, 6):
+                self.send(j, chunk).wait_send()
+
+            @pl.when(at.inner)
+            def _():
+                self.send(4, chunk).wait_send()
+
+            @pl.when(at.outer)
+            def _():
+                self.send(2, chunk).wait_send()
+
+
+def tree_scratch(count, n, width):
+    return [pltpu.VMEM((count, n // part, width), bf16) for part in (1, 2, 4, 8)] + [
+        pltpu.SemaphoreType.DMA((8, count)),
+        pltpu.SemaphoreType.DMA((8, count)),
+        pltpu.SemaphoreType.DMA((count,)),
+    ]
+
+
+def plane_scratch(count, n, width):
+    return [pltpu.VMEM((count, n // part, width), bf16) for part in (2, 4, 4, 4)] + [
+        pltpu.SemaphoreType.DMA((7, count)),
+        pltpu.SemaphoreType.DMA((7, count)),
+        pltpu.SemaphoreType.DMA((count,)),
+    ]
+
+
+def advance(tick, count, sums):
+    for k in reversed(range(max(s.steps for s in sums))):
+        chunk = tick - k
+
+        @pl.when((chunk >= 0) & (chunk < count))
+        def _():
+            for s in sums:
+                if k < s.steps:
+                    s.step(k, chunk)
+
+
+def dot(left, right, contract):
+    return lax.dot_general(left, right, (contract, ((), ())), preferred_element_type=f32)
+
+
+NN = ((1,), (0,))
+NT = ((1,), (1,))
+TN = ((0,), (0,))
+
+
+def gelu_and_slope(u):
+    c = 0.7978845608028654
+    square = u * u
+    t = jnp.tanh(c * u * (1.0 + 0.044715 * square))
+    half = 0.5 * (1.0 + t)
+    slope = half + 0.5 * u * (1.0 - t * t) * (c * (1.0 + 3 * 0.044715 * square))
+    return u * half, slope
+
+
+def ff_kernel(
+    h2_ref,
+    x2_ref,
+    og_ref,
+    wup_ref,
+    wdown_ref,
+    bup_ref,
+    bdown_ref,
+    out_ref,
+    dh2_ref,
+    g1_ref,
+    g2_ref,
+    dbup_ref,
+    h2,
+    h2t,
+    og,
+    out,
+    dh2,
+    wu,
+    wd,
+    bup,
+    bdown,
+    dbup,
+    out16,
+    mine1,
+    mine2,
+    sib1,
+    sib2,
+    sum1,
+    sum2,
+    *rest,
+):
+    rest = list(rest)
+    local, wsem, gsent, ggot = rest[:4]
+    tree, plane1, plane2 = rest[4:11], rest[11:18], rest[18:25]
+    at = Place()
+    loads = [
+        pltpu.make_async_copy(s, d, local.at[j])
+        for j, (s, d) in enumerate(
+            ((h2_ref, h2), (og_ref, og), (x2_ref, out), (bup_ref, bup), (bdown_ref, bdown))
+        )
+    ]
+    for load in loads:
+        load.start()
+
+    def weights(i, slot):
+        cols = [pl.ds(aligned(h * TILES * TILE + i * TILE, TILE), TILE) for h in (0, 1)]
+        parts = []
+        for h in (0, 1):
+            here = pl.ds(h * TILE, TILE)
+            parts.append(
+                pltpu.make_async_copy(
+                    wup_ref.at[:, cols[h]], wu.at[slot, :, here], wsem.at[h, slot]
+                )
+            )
+            parts.append(
+                pltpu.make_async_copy(
+                    wdown_ref.at[cols[h], :], wd.at[slot, here, :], wsem.at[2 + h, slot]
+                )
+            )
+        return parts
+
+    for part in weights(0, 0):
+        part.start()
+    at.barrier()
+    for load in loads:
+        load.wait()
+    for b in range(8):
+        rows = pl.ds(b * 128, 128)
+        h2t[:, rows] = h2[rows, :].T
+    out[...] = out[...] + bdown[...].astype(f32)
+    dh2[...] = jnp.zeros_like(dh2)
+
+    sums = [
+        TreeFirst(at, sum1, g1_ref, tree[:4], *tree[4:]),
+        PlaneFirst(at, sum2, g2_ref, 0, FIRST, True, plane1[:4], *plane1[4:]),
+        PlaneFirst(at, sum2, g2_ref, FIRST, SECOND, False, plane2[:4], *plane2[4:]),
+    ]
+
+    def to_sibling(slot):
+        return (
+            at.copy_sibling(
+                mine1.at[slot, 1 - at.core], sib1.at[slot], gsent.at[0, slot], ggot.at[0, slot]
+            ),
+            at.copy_sibling(
+                mine2.at[slot, 1 - at.core], sib2.at[slot], gsent.at[1, slot], ggot.at[1, slot]
+            ),
+        )
+
+    def meet(i):
+        slot = lax.rem(i, 2)
+        for copy in to_sibling(slot):
+            copy.wait()
+        sum1[i] = (mine1[slot, at.core].astype(f32) + sib1[slot].astype(f32)).astype(bf16)
+        sum2[i] = (mine2[slot, at.core].astype(f32) + sib2[slot].astype(f32)).astype(bf16)
+
+    def compute(i):
+        slot = lax.rem(i, 2)
+        for part in weights(i, slot):
+            part.wait()
+
+        @pl.when(i + 1 < TILES)
+        def _():
+            for part in weights(i + 1, 1 - slot):
+                part.start()
+
+        bias = bup[i].astype(f32)
+        u = dot(h2[...], wu[slot], NN) + bias
+        a, slope = gelu_and_slope(u)
+        a = a.astype(bf16)
+        out[...] += dot(a, wd[slot], NN)
+        d_wd = dot(a, og[...], TN).astype(bf16)
+        mine1[slot, 0] = d_wd[:TILE]
+        mine1[slot, 1] = d_wd[TILE:]
+        du = (dot(og[...], wd[slot], NT) * slope).astype(bf16)
+        d_wu = dot(h2t[...], du, NN).astype(bf16)
+        mine2[slot, 0] = d_wu[:HALF]
+        mine2[slot, 1] = d_wu[HALF:]
+        for copy in to_sibling(slot):
+            copy.start()
+        dh2[...] += dot(du, wu[slot], NT)
+        dbup[i] = jnp.sum(du.astype(f32), axis=0, keepdims=True)
+
+    def body(i, carry):
+        @pl.when((i >= 1) & (i <= TILES))
+        def _():
+            meet(i - 1)
+
+        advance(i - 1, TILES, sums)
+
+        @pl.when(i < TILES)
+        def _():
+            compute(i)
+
+        @pl.when(i == TILES)
+        def _():
+            out16[...] = out[...].astype(bf16)
+            pltpu.make_async_copy(out16, out_ref, local.at[0]).start()
+            pltpu.make_async_copy(dh2, dh2_ref, local.at[1]).start()
+            pltpu.make_async_copy(dbup, dbup_ref, local.at[2]).start()
+
+        return carry
+
+    lax.fori_loop(0, TILES + 1 + 8, body, 0)
+    pltpu.make_async_copy(out16, out_ref, local.at[0]).wait()
+    pltpu.make_async_copy(dh2, dh2_ref, local.at[1]).wait()
+    pltpu.make_async_copy(dbup, dbup_ref, local.at[2]).wait()
+
+def feed_forward(h2, x2, og, wup, wdown, bup, bdown):
+    rows = h2.shape[0]
+    return pl.pallas_call(
+        ff_kernel,
+        out_shape=(
+            jax.ShapeDtypeStruct((rows, WIDTH), bf16),
+            jax.ShapeDtypeStruct((rows, WIDTH), f32),
+            jax.ShapeDtypeStruct((TILES, TILE, WIDTH), bf16),
+            jax.ShapeDtypeStruct((TILES, HALF, 2 * TILE), bf16),
+            jax.ShapeDtypeStruct((TILES, 1, 2 * TILE), f32),
+        ),
+        in_specs=[ANY] * 7,
+        out_specs=[ANY] * 5,
+        scratch_shapes=[
+            pltpu.VMEM((rows, WIDTH), bf16),
+            pltpu.VMEM((WIDTH, rows), bf16),
+            pltpu.VMEM((rows, WIDTH), bf16),
+            pltpu.VMEM((rows, WIDTH), f32),
+            pltpu.VMEM((rows, WIDTH), f32),
+            pltpu.VMEM((2, WIDTH, 2 * TILE), bf16),
+            pltpu.VMEM((2, 2 * TILE, WIDTH), bf16),
+            pltpu.VMEM((TILES, 1, 2 * TILE), bf16),
+            pltpu.VMEM((1, WIDTH), bf16),
+            pltpu.VMEM((TILES, 1, 2 * TILE), f32),
+            pltpu.VMEM((rows, WIDTH), bf16),
+            pltpu.VMEM((2, 2, TILE, WIDTH), bf16),
+            pltpu.VMEM((2, 2, HALF, 2 * TILE), bf16),
+            pltpu.VMEM((2, TILE, WIDTH), bf16),
+            pltpu.VMEM((2, HALF, 2 * TILE), bf16),
+            pltpu.VMEM((TILES, TILE, WIDTH), bf16),
+            pltpu.VMEM((TILES, HALF, 2 * TILE), bf16),
+            pltpu.SemaphoreType.DMA((5,)),
+            pltpu.SemaphoreType.DMA((4, 2)),
+            pltpu.SemaphoreType.DMA((2, 2)),
+            pltpu.SemaphoreType.DMA((2, 2)),
+        ]
+        + tree_scratch(TILES, TILE, WIDTH)
+        + plane_scratch(TILES, FIRST, 2 * TILE)
+        + plane_scratch(TILES, SECOND, 2 * TILE),
+        compiler_params=pltpu.CompilerParams(
+            collective_id=1, has_side_effects=True, vmem_limit_bytes=62 * 2**20
+        ),
+        name="feed_forward",
+    )(h2, x2, og, wup, wdown, bup, bdown)
+
+
+CHUNKS = 9
+
+
+def attention_sum_kernel(grad_ref, out_ref, sum1, sum2, sib1, sib2, *rest):
+    rest = list(rest)
+    local, gsent, ggot = rest[:3]
+    tree, plane1, plane2 = rest[3:10], rest[10:17], rest[17:24]
+    at = Place()
+    own = [
+        pltpu.make_async_copy(grad_ref.at[at.core, j], s, local.at[j])
+        for j, s in ((0, sum1), (1, sum2))
+    ]
+    for load in own:
+        load.start()
+    at.barrier()
+
+    def sibling(j, chunk):
+        return at.copy_sibling(
+            grad_ref.at[1 - at.core, j, chunk],
+            (sib1, sib2)[j].at[chunk],
+            gsent.at[j, chunk],
+            ggot.at[j, chunk],
+        )
+
+    for chunk in range(CHUNKS):
+        sibling(0, chunk).start()
+        sibling(1, chunk).start()
+    for load in own:
+        load.wait()
+    sums = [
+        TreeFirst(at, sum1, out_ref.at[0], tree[:4], *tree[4:]),
+        PlaneFirst(at, sum2, out_ref.at[1], 0, TILE // 2, True, plane1[:4], *plane1[4:]),
+        PlaneFirst(
+            at, sum2, out_ref.at[1], TILE // 2, TILE // 2, False, plane2[:4], *plane2[4:]
+        ),
+    ]
+
+    def body(i, carry):
+        @pl.when(i < CHUNKS)
+        def _():
+            sibling(0, i).wait()
+            sibling(1, i).wait()
+            sum1[i] = (sum1[i].astype(f32) + sib1[i].astype(f32)).astype(bf16)
+            sum2[i] = (sum2[i].astype(f32) + sib2[i].astype(f32)).astype(bf16)
+
+        advance(i, CHUNKS, sums)
+        return carry
+
+    lax.fori_loop(0, CHUNKS + 8, body, 0)
+
+def attention_sum(grads):
+    return pl.pallas_call(
+        attention_sum_kernel,
+        out_shape=jax.ShapeDtypeStruct((2, CHUNKS, TILE, WIDTH), bf16),
+        in_specs=[ANY],
+        out_specs=ANY,
+        scratch_shapes=[pltpu.VMEM((CHUNKS, TILE, WIDTH), bf16)] * 4
+        + [
+            pltpu.SemaphoreType.DMA((2,)),
+            pltpu.SemaphoreType.DMA((2, CHUNKS)),
+            pltpu.SemaphoreType.DMA((2, CHUNKS)),
+        ]
+        + tree_scratch(CHUNKS, TILE, WIDTH)
+        + plane_scratch(CHUNKS, TILE // 2, WIDTH)
+        + plane_scratch(CHUNKS, TILE // 2, WIDTH),
+        compiler_params=pltpu.CompilerParams(
+            collective_id=2, has_side_effects=True, vmem_limit_bytes=62 * 2**20
+        ),
+        name="attention_sum",
+    )(grads)
+
+
+def gather(value):
+    return lax.all_gather(value, "group", axis=0, tiled=True)
+
+
+def fast_shards(
+    tokens,
+    out_grad,
+    ln1_gain,
+    ln1_bias,
+    q_weight,
+    q_bias,
+    k_weight,
+    v_weight,
+    v_bias,
+    o_weight,
+    o_bias,
+    ln2_gain,
+    ln2_bias,
+    up_weight,
+    up_bias,
+    down_weight,
+    down_bias,
+):
+    gap = TILES * TILE - FF_HALF
+    gain_one, shift_one, wq, bq, wk, wv, bv, wo, bo, gain_two, shift_two, bdown = [
+        gather(v)
+        for v in (
+            ln1_gain,
+            ln1_bias,
+            q_weight,
+            q_bias,
+            k_weight,
+            v_weight,
+            v_bias,
+            o_weight,
+            o_bias,
+            ln2_gain,
+            ln2_bias,
+            down_bias,
+        )
+    ]
+    up_parts = jnp.pad(up_weight.reshape(HALF, 2, FF_HALF), ((0, 0), (0, 0), (0, gap)))
+    wup = gather(up_parts.reshape(HALF, FF_PAD))
+    wdown = gather(jnp.pad(down_weight, ((0, gap), (0, 0))))
+    bup = gather(jnp.pad(up_bias, (0, gap)))
+    bup = bup.reshape(2, TILES, TILE).transpose(1, 0, 2).reshape(TILES, 1, 2 * TILE)
+
+    input_f = tokens.astype(f32)
+    gain_one, shift_one = gain_one.astype(f32), shift_one.astype(f32)
+    gain_two, shift_two = gain_two.astype(f32), shift_two.astype(f32)
+    normed1 = layer_norm(input_f, gain_one, shift_one).astype(bf16)
+    query = (jnp.dot(normed1, wq, preferred_element_type=f32) + bq.astype(f32)).astype(bf16)
+    key_rows = jnp.dot(normed1, wk, preferred_element_type=f32).astype(bf16)
+    value_rows = (jnp.dot(normed1, wv, preferred_element_type=f32) + bv.astype(f32)).astype(bf16)
+    mixed, log_total = attend(query, key_rows, value_rows)
+    attn_in = mixed.astype(bf16)
+    residual = input_f + jnp.dot(attn_in, wo, preferred_element_type=f32) + bo.astype(f32)
+    normed2 = layer_norm(residual, gain_two, shift_two).astype(bf16)
+
+    output, d_normed2, g1, g2, d_bup = feed_forward(
+        normed2, residual, out_grad, wup, wdown, bup, bdown.reshape(1, WIDTH)
+    )
+
+    _, norm_back_two = jax.vjp(layer_norm, residual, gain_two, shift_two)
+    d_res_norm, d_gain_two, d_shift_two = norm_back_two(d_normed2)
+    d_residual = out_grad.astype(f32) + d_res_norm
+    d_attn = d_residual.astype(bf16)
+    d_wout = outer_rows(attn_in, d_attn)
+    d_mixed = back_rows(d_attn, wo).astype(bf16)
+    d_query, d_key, d_value = attend_back(query, key_rows, value_rows, log_total, d_mixed)
+    d_wquery = outer_rows(normed1, d_query)
+    d_wkey = outer_rows(normed1, d_key)
+    d_wvalue = outer_rows(normed1, d_value)
+    d_normed1 = back_rows(d_query, wq) + back_rows(d_key, wk) + back_rows(d_value, wv)
+    _, norm_back_one = jax.vjp(layer_norm, input_f, gain_one, shift_one)
+    d_in_norm, d_gain_one, d_shift_one = norm_back_one(d_normed1)
+    d_input = (d_residual + d_in_norm).astype(bf16)
+
+    parts = [w.astype(bf16).reshape(2, 1, HALF, WIDTH) for w in (d_wquery, d_wkey, d_wvalue, d_wout)]
+    grads = jnp.concatenate(parts, axis=1).reshape(2, 2, CHUNKS, TILE, WIDTH)
+    g3 = attention_sum(grads).reshape(4, HALF, WIDTH)
+
+    d_bup = d_bup.reshape(TILES, 2, TILE).transpose(1, 0, 2).reshape(2, TILES * TILE)[:, :FF_HALF]
+    small = [
+        d_gain_one,
+        d_shift_one,
+        column_sums(d_query),
+        column_sums(d_value),
+        column_sums(d_attn),
+        d_gain_two,
+        d_shift_two,
+        column_sums(out_grad),
+    ]
+    pack = jnp.concatenate([v.reshape(2, HALF) for v in small] + [d_bup], axis=1).astype(bf16)
+    pack = lax.psum(pack, ("group", "replica")).astype(f32)
+    mine = lax.dynamic_index_in_dim(pack, lax.axis_index("group"), 0, keepdims=False)
+    small = [mine[j * HALF : (j + 1) * HALF] for j in range(8)]
+
+    g1 = g1.reshape(TILES * TILE, WIDTH)[:FF_HALF].astype(f32)
+    g2 = g2.reshape(TILES, HALF, 2, TILE).transpose(1, 2, 0, 3).reshape(HALF, 2, TILES * TILE)
+    g2 = g2[:, :, :FF_HALF].reshape(HALF, FF).astype(f32)
+    g3 = g3.astype(f32)
+    return (
+        output,
+        d_input,
+        small[0],
+        small[1],
+        g3[0],
+        small[2],
+        g3[1],
+        g3[2],
+        small[3],
+        g3[3],
+        small[4],
+        small[5],
+        small[6],
+        g2,
+        mine[8 * HALF :],
+        g1,
+        small[7],
+    )
+
+
 def solution(mesh):
     placed = (
         P(("group", "replica"), None),
@@ -289,8 +1015,9 @@
         P("group", None),
         P("group"),
     )
+    fast = mesh.shape["group"] == 2 and mesh.shape["replica"] == 16
     return jax.shard_map(
-        shards,
+        fast_shards if fast else shards,
         mesh=mesh,
         in_specs=placed,
         out_specs=(

time: 827 us -> 717 us (0.87)
  Pallas kernels: 0 us -> 344 us
  waiting for transfers between devices: 298 us -> 2.64 us
  matrix products: 233 us -> 91.9 us
  blocking collectives: 106 us -> 44.3 us
  local copies, waits for them, and re-layouts: 115 us -> 159 us
    pallas_call x0 -> x2, Pallas kernels: none -> 344 us  [the longest x1 220 us: feed_forward(): pl.pallas_call(ff_kernel, out_shape=(jax.ShapeDtypeStruct((rows, WIDTH),...]
    psum x1 -> x0, waiting for transfers between devices: 291 us -> none  [shards(): lax.psum(attn_grads[2].astype(jnp.bfloat16), 'replica').astype(jnp.float32)]
    dot_general x6 -> x4, matrix products: 72.5 us -> 17.4 us  [back_rows(): jnp.einsum('rb,ab->ra', grads, weight, preferred_element_type=jnp.float32)]
    dot_general x6 -> x4, matrix products: 72.4 us -> 27.6 us  [the longest x1 7.32 us: fast_shards(): jnp.dot(normed1, wv, preferred_element_type=f32) + bv.astype(f32)]
    psum x1, blocking collectives: 81.5 us -> 38.6 us  [fast_shards(): pack = lax.psum(pack, ('group', 'replica')).astype(f32)]
    dot_general x6 -> x4, matrix products: 59.8 us -> 20.7 us  [outer_rows(): jnp.einsum('ra,rb->ab', left, right, preferred_element_type=jnp.float32)]
    reshape x0 -> x15, local copies, waits for them, and re-layouts: none -> 33.6 us  [the longest x2 22.7 us: fast_shards(): g2.reshape(TILES, HALF, 2, TILE).transpose(1, 2, 0, 3)]
    unnamed x3 -> x1, blocking collectives: 24.3 us -> 3.69 us
  transfers between devices with their start and end apart: 13 -> 6, of which waited for: 3 -> 0; matrix products, arithmetic and copies ran while one was open for 34% -> 17% of each run, Pallas kernels for 0% -> 0%
where the time goes in v1:
time: 717 us; the launch traced here: 708 us
  Pallas kernels  344 us (48%)
  local copies, waits for them, and re-layouts  159 us (22%)
  matrix products  91.9 us (13%)
  other arithmetic  50 us (7%)
  blocking collectives  44.3 us (6%)
  between operations  15.9 us (2%)
    pallas_call x1, Pallas kernels, feed_forward(): pl.pallas_call(ff_kernel, out_shape=(jax.ShapeDtypeStruct((rows, WIDTH),...  220 us
    pallas_call x1, Pallas kernels, attention_sum(): pl.pallas_call(attention_sum_kernel, out_shape=jax.ShapeDtypeStruct((2, C...  124 us
    reshape x8, local copies, waits for them, and re-layouts, split_heads(): return rows.reshape(-1, PATCHES, HEADS, rows.shape[-1] // HEADS)  61.4 us
    psum x1, blocking collectives, fast_shards(): pack = lax.psum(pack, ('group', 'replica')).astype(f32)  38.6 us
    unnamed x101, local copies, waits for them, and re-layouts  28.6 us
    reshape x2, local copies, waits for them, and re-layouts, fast_shards(): g2.reshape(TILES, HALF, 2, TILE).transpose(1, 2, 0, 3)  22.7 us
    dot_general x4, matrix products, outer_rows(): jnp.einsum('ra,rb->ab', left, right, preferred_element_type=jnp.float32)  20.7 us
    dot_general x4, matrix products, back_rows(): jnp.einsum('rb,ab->ra', grads, weight, preferred_element_type=jnp.float32)  17.4 us
  transfers between devices with their start and end apart: 6, of which 0 were waited for; matrix products, arithmetic and copies ran while one was open for 17% of the time, Pallas kernels for 0%

profile of v1, /device:TPU:0, one launch (start us, length us, event | category | flops | bytes accessed | tf_op | source)
XLA Modules:
  0.0 707.8 jit_solution(10086458668623003135)
XLA Ops:
  10.0 5.0 pad.13
  15.1 8.9 %reshape.242 = bf16[576,2,2152]{2,1,0:T(2,128)(2,1)} reshape(bf16[576,4304]{1,0:T(8,128)(2,1)} %param.30) | data formatting | bytes 9916416 | tf_op jit(solution)/shard_map/reshape | solution.py:916
  24.0 8.6 %pad.12 = bf16[576,2,2176]{2,1,0:T(2,128)(2,1)} pad(bf16[576,2,2152]{2,1,0:T(2,128)(2,1)} %reshape.242, bf16[]{:T(256)} %constant.30.clone.1), padding=0_0x0_0x0_24 | pad | bytes 9971714 | tf_op jit(solution)/shard_map/jit(_pad)/pad | solution.py:916
  32.7 6.0 copy.119
  42.6 3.7 all-reduce.11
  51.0 6.9 add_convert_fusion.2
  57.8 9.6 %reshape.316 = bf16[8,128,16,72]{3,2,1,0:T(8,128)(2,1)} reshape(bf16[1024,1152]{1,0:T(8,128)(2,1)} %add_convert_fusion.2) | data formatting | bytes 4718592 | tf_op jit(solution)/shard_map/reshape | solution.py:25
  67.4 6.2 copy.81
  73.6 7.3 %add_convert_fusion.3 = bf16[1024,1152]{1,0:T(8,128)(2,1)} fusion(bf16[1152,1152]{1,0:T(8,128)(2,1)} %all-gather.8.cloned.1.call-done, f32[1152]{0:T(1024)S(1)} %convert_element_type.138, bf16[1024,1152]{1,0:T(8,128)(2,1)S(1)} %copy-done.3, f32[1152]{0:T(1024)S(1)} %convert_element_type.136, f32[1152]{0:T(1024)S(1)} %convert_element_type.135, ...), kind=kOutput, calls=%fused_computation.40 | convolution fusion | flops 2727346176 | bytes 7394816 | tf_op jit(solution)/shard_map/dot_general | solution.py:928
  80.9 9.6 %reshape.315 = bf16[8,128,16,72]{3,2,1,0:T(8,128)(2,1)} reshape(bf16[1024,1152]{1,0:T(8,128)(2,1)} %add_convert_fusion.3) | data formatting | bytes 4718592 | tf_op jit(solution)/shard_map/reshape | solution.py:25
  90.5 6.2 copy.83
  96.7 6.8 convolution_convert_fusion.5
  103.6 9.7 %reshape.317 = bf16[8,128,16,72]{3,2,1,0:T(8,128)(2,1)} reshape(bf16[1024,1152]{1,0:T(8,128)(2,1)} %convolution_convert_fusion.5) | data formatting | bytes 4718592 | tf_op jit(solution)/shard_map/reshape | solution.py:25
  113.2 6.5 copy.82
  119.8 4.0 multiply_reduce_fusion.1
  131.8 6.6 fusion.51
  142.9 220.0 %feed_forward.1 = (bf16[1024,1152]{1,0:T(8,128)(2,1)}, f32[1024,1152]{1,0:T(8,128)}, bf16[17,128,1152]{2,1,0:T(8,128)(2,1)}, bf16[17,576,256]{2,1,0:T(8,128)(2,1)}, f32[17,1,256]{2,1,0:T(1,128)}) custom-call(bf16[1024,1152]{1,0:T(8,128)(2,1)} %add_convert_fusion.1.h2_ref, f32[1024,1152]{1,0:T(8,128)} %copy-done.1, bf16[1024,1152]{1,0:T(8,128)(2,1)} %og_ref.1, ...), custom_call_target="tpu_custom_call" | custom-call | tf_op jit(solution)/shard_map/feed_forward/pallas_call | solution.py:759
  362.9 5.1 multiply_reduce_fusion.2
  374.7 4.5 convolution_convert_fusion
  379.2 4.0 convolution_convert_fusion.4
  383.2 8.3 %reshape.318 = bf16[8,128,16,72]{3,2,1,0:T(8,128)(2,1)} reshape(bf16[1024,1152]{1,0:T(8,128)(2,1)S(1)} %convolution_convert_fusion.4) | data formatting | bytes 4718592 | tf_op jit(solution)/shard_map/reshape | solution.py:25
  391.5 5.3 copy.89
  396.8 8.1 %fusion.53 = (bf16[16,72]{1,0:T(8,128)(2,1)S(1)}, bf16[8,128,16,72]{1,3,2,0:T(8,128)(2,1)}) fusion(bf16[8,128,16,72]{1,3,2,0:T(8,128)(2,1)S(1)} %copy.89, f32[8,16,128,128]{2,3,1,0:T(8,128)} %copy-done, f32[8,16,128]{2,1,0:T(8,128)S(1)} %log_add_fusion), kind=kOutput, calls=%fused_computation.100 | convolution fusion | flops 310639488 | bytes 13175040 | tf_op jit(solution)/shard_map/ihst,isha->itha/dot_general | solution.py:64
  404.9 5.1 multiply_reduce_fusion
  410.0 3.0 multiply_convert_fusion
  413.1 4.5 fusion.15
  417.6 2.9 fusion.52
  421.0 3.2 copy.99
  424.2 5.2 convolution_convert_fusion.1
  429.5 3.2 copy.96
  432.8 5.4 convolution_convert_fusion.2
  439.9 3.6 fusion.19
  443.5 3.6 fusion.22
  447.1 6.3 fusion.47
  453.5 4.1 fusion.9
  457.8 38.6 %psum.7 = bf16[2,6760]{1,0:T(2,128)(2,1)S(1)} all-reduce(bf16[2,6760]{1,0:T(2,128)(2,1)S(1)} %concatenate.7), channel_id=1, replica_groups=mesh['group'=2,'replica'=16] {'group','replica'}, use_global_device_ids=true, to_apply=%region_19.20 | all-reduce | flops 13520 | bytes 54080 | tf_op jit(solution)/shard_map/psum | solution.py:969
  497.8 5.6 convolution_convert_fusion.3
  503.4 5.1 add_convert_fusion
  508.7 5.1 pad_maximum_fusion
  513.8 123.8 %attention_sum.1 = bf16[2,9,128,1152]{3,2,1,0:T(8,128)(2,1)} custom-call(bf16[2,2,9,128,1152]{4,3,2,1,0:T(8,128)(2,1)} %bitcast.108), custom_call_target="tpu_custom_call" | custom-call | tf_op jit(solution)/shard_map/attention_sum/pallas_call | solution.py:854
  637.5 10.3 %reshape.266 = bf16[17,576,2,128]{3,2,1,0:T(2,128)(2,1)} reshape(bf16[17,576,256]{2,1,0:T(8,128)(2,1)} %get-tuple-element.25) | data formatting | bytes 10027008 | tf_op jit(solution)/shard_map/reshape | solution.py:974
  647.8 12.4 %copy.104 = bf16[17,576,2,128]{1,3,0,2:T(8,128)(2,1)} copy(bf16[17,576,2,128]{3,2,1,0:T(2,128)(2,1)} %reshape.266) | data formatting | bytes 10027008 | tf_op jit(solution)/shard_map/reshape | solution.py:974
  660.2 5.5 slice.113
  665.7 3.2 convert.54
  668.9 4.2 slice_bitcast_fusion
  673.1 7.4 %bitcast_convert_fusion = f32[576,4304]{0,1:T(8,128)} fusion(bf16[576,2,2152]{0,2,1:T(8,128)(2,1)} %slice.113), kind=kLoop, calls=%fused_computation.19 | loop fusion | flops 2479104 | bytes 14874624 | tf_op jit(solution)/shard_map/convert_element_type | solution.py:975
  680.5 11.5 %copy.105 = f32[576,4304]{1,0:T(8,128)} copy(f32[576,4304]{0,1:T(8,128)} %bitcast_convert_fusion) | data formatting | bytes 19832832
  692.1 7.1 %slice_convert_fusion = f32[2152,1152]{1,0:T(8,128)} fusion(bf16[2176,1152]{1,0:T(8,128)(2,1)} %bitcast.115), kind=kLoop, calls=%fused_computation.23 | loop fusion | flops 2479104 | bytes 14874624 | tf_op jit(solution)/shard_map/convert_element_type | solution.py:973
  (165 shorter events, 35.3 us)
Async XLA Ops:
  7.2 43.8 %all-gather.10.cloned.1.call-start = ((), (), s32[]{:S(2)}) async-start(), calls=%async_computation.1 | async-start | bytes 3981312 | tf_op jit(solution)/shard_map/all_gather | solution.py:876
  7.9 65.7 %all-gather.8.cloned.1.call-start = ((), (), s32[]{:S(2)}) async-start(), calls=%async_computation | async-start | bytes 3981312 | tf_op jit(solution)/shard_map/all_gather | solution.py:876
  8.7 88.0 %all-gather.12.cloned.1.call-start = ((), (), s32[]{:S(2)}) async-start(), calls=%async_computation.2 | async-start | bytes 3981312 | tf_op jit(solution)/shard_map/all_gather | solution.py:876
  9.4 122.4 %all-gather.14.cloned.1.call-start = ((), (), s32[]{:S(2)}) async-start(), calls=%async_computation.3 | async-start | bytes 3981312 | tf_op jit(solution)/shard_map/all_gather | solution.py:876
  10.0 133.0 %all-gather.18.cloned.1.call-start = ((), (), s32[]{:S(2)}) async-start(), calls=%async_computation.5 | async-start | bytes 15040512 | tf_op jit(solution)/shard_map/all_gather | solution.py:876
  15.0 127.9 %all-gather.16.cloned.1.call-start = ((), (), s32[]{:S(2)}) async-start(), calls=%async_computation.4 | async-start | bytes 15040512 | tf_op jit(solution)/shard_map/all_gather | solution.py:876
  38.7 0.7 copy-start.37
  38.7 1.9 copy-start.26
  38.7 2.2 copy-start.27
  38.7 2.4 copy-start.28
  38.7 2.6 copy-start.29
  38.8 2.9 copy-start.30
  38.8 3.1 copy-start.31
  38.8 3.3 copy-start.32
  38.8 3.6 copy-start.33
  38.8 8.1 %copy-start.25 = (bf16[2152]{0:T(1024)(128)(2,1)S(1)}, bf16[2152]{0:T(1024)(128)(2,1)}, u32[]{:S(2)}) copy-start(bf16[2152]{0:T(1024)(128)(2,1)} %param.31) | copy-start | bytes 12916
  38.8 10.9 %copy-start.3 = (bf16[1024,1152]{1,0:T(8,128)(2,1)S(1)}, bf16[1024,1152]{1,0:T(8,128)(2,1)}, u32[]{:S(2)}) copy-start(bf16[1024,1152]{1,0:T(8,128)(2,1)} %param.17) | copy-start | bytes 7077892
  123.8 5.1 copy-start
  123.8 3.4 copy-start.10
  138.4 2.2 copy-start.1
  362.9 5.2 copy-start.2
  362.9 6.5 copy-start.13
  369.4 1.9 copy-start.6
  371.3 2.4 copy-start.5
  371.3 3.4 copy-start.14
  374.7 4.5 copy-start.16
  396.8 8.1 %copy-start.11 = (bf16[8,128,16,72]{1,3,2,0:T(8,128)(2,1)S(1)}, bf16[8,128,16,72]{1,3,2,0:T(8,128)(2,1)}, u32[]{:S(2)}) copy-start(bf16[8,128,16,72]{1,3,2,0:T(8,128)(2,1)} %copy.83) | copy-start | bytes 7077892
  396.8 13.2 %slice-start = ((s8[8388608]{0:T(1024)(128)(4,1)}), s8[4194304]{0:T(1024)(128)(4,1)S(1)}, s32[]{:S(2)}) async-start(s8[8388608]{0:T(1024)(128)(4,1)} %bitcast.106), calls=%async_computation.6 | async-start | bytes 8388608
  404.9 5.1 slice-start.1
  410.0 3.0 copy-start.8
  413.1 4.5 copy-start.9
  417.6 2.9 copy-start.24
  417.6 6.7 copy-start.4
  424.2 5.3 copy-start.22
  432.7 5.4 copy-start.15
  438.2 1.7 copy-start.36
  439.9 3.6 copy-start.21
  439.9 3.6 copy-start.34
  443.5 3.6 copy-start.23
  443.5 3.6 copy-start.35
  497.8 5.6 copy-start.7
  497.8 5.6 copy-start.12
  503.4 5.1 copy-start.17
  503.4 5.1 copy-start.18
  503.4 5.3 copy-start.19
  692.0 7.1 %copy-start.20 = (bf16[1024,1152]{1,0:T(8,128)(2,1)S(1)}, bf16[1024,1152]{1,0:T(8,128)(2,1)}, u32[]{:S(2)}) copy-start(bf16[1024,1152]{1,0:T(8,128)(2,1)} %get-tuple-element.121) | copy-start | bytes 7077892
Sparse Core Ops, SparseCore 0:
  9.6 14.0 all-gather.9
  25.2 12.5 all-gather.7
  39.4 12.5 all-gather.11
  53.4 12.5 all-gather.13
  67.4 23.5 all-gather.17
  92.5 23.5 all-gather.15

commit v2 on v1

--- a/solution.py
+++ b/solution.py
@@ -676,7 +676,7 @@
     for b in range(8):
         rows = pl.ds(b * 128, 128)
         h2t[:, rows] = h2[rows, :].T
-    out[...] = out[...] + bdown[...].astype(f32)
+    out[...] = out[...] + bdown[7:8, :]
     dh2[...] = jnp.zeros_like(dh2)
 
     sums = [
@@ -712,7 +712,7 @@
             for part in weights(i + 1, 1 - slot):
                 part.start()
 
-        bias = bup[i].astype(f32)
+        bias = jnp.concatenate([bup[0, i], bup[1, i]], axis=1)
         u = dot(h2[...], wu[slot], NN) + bias
         a, slope = gelu_and_slope(u)
         a = a.astype(bf16)
@@ -775,8 +775,8 @@
             pltpu.VMEM((rows, WIDTH), f32),
             pltpu.VMEM((2, WIDTH, 2 * TILE), bf16),
             pltpu.VMEM((2, 2 * TILE, WIDTH), bf16),
-            pltpu.VMEM((TILES, 1, 2 * TILE), bf16),
-            pltpu.VMEM((1, WIDTH), bf16),
+            pltpu.VMEM((2, TILES, 1, TILE), f32),
+            pltpu.VMEM((VECTORS, WIDTH), f32),
             pltpu.VMEM((TILES, 1, 2 * TILE), f32),
             pltpu.VMEM((rows, WIDTH), bf16),
             pltpu.VMEM((2, 2, TILE, WIDTH), bf16),
@@ -872,8 +872,329 @@
     )(grads)
 
 
-def gather(value):
-    return lax.all_gather(value, "group", axis=0, tiled=True)
+VECTORS = 8
+LANES = 640
+SCALE = 72**-0.5
+HEAD = 72
+
+
+def head_window(h):
+    return slice(h * HEAD // 128 * 128, ((h + 1) * HEAD + 127) // 128 * 128)
+
+
+def only_head(rows, h):
+    lane = lax.broadcasted_iota(jnp.int32, rows.shape, 1) + head_window(h).start
+    return jnp.where((lane >= h * HEAD) & (lane < (h + 1) * HEAD), rows, jnp.zeros_like(rows))
+
+
+class Lanes:
+    def __init__(self):
+        self.tiles = [None] * (WIDTH // 128)
+
+    def add(self, h, window):
+        first = head_window(h).start // 128
+        for j in range(window.shape[1] // 128):
+            part = window[:, j * 128 : (j + 1) * 128]
+            old = self.tiles[first + j]
+            self.tiles[first + j] = part if old is None else old + part
+
+    def joined(self):
+        return jnp.concatenate([t.astype(bf16) for t in self.tiles], axis=1)
+
+
+def normalise(rows, gain, shift):
+    center = rows - jnp.mean(rows, axis=-1, keepdims=True)
+    spread = jnp.mean(center * center, axis=-1, keepdims=True)
+    return center * lax.rsqrt(spread + 1e-06) * gain + shift
+
+
+def forward_kernel(
+    tokens_ref,
+    wq_ref,
+    wk_ref,
+    wv_ref,
+    wo_ref,
+    up_ref,
+    down_ref,
+    pack_ref,
+    bup_ref,
+    h1_ref,
+    q_ref,
+    k_ref,
+    v_ref,
+    ao_ref,
+    probs_ref,
+    x2_ref,
+    h2_ref,
+    w_ref,
+    wup_ref,
+    wdown_ref,
+    vec_ref,
+    bups_ref,
+    x,
+    h1,
+    q,
+    k,
+    v,
+    ao,
+    probs,
+    x2,
+    h2,
+    w,
+    up,
+    up_wide,
+    zeros,
+    pack,
+    vec,
+    local,
+    wsem,
+    psem,
+    sent,
+    got,
+    bsem,
+):
+    at = Place()
+    core = at.core
+    own = pl.ds(aligned(core * HALF, HALF), HALF)
+    ff_own = pl.ds(aligned(core * TILES * TILE, TILE), FF_HALF)
+    shards = (wq_ref, wk_ref, wv_ref, wo_ref)
+    load_x = pltpu.make_async_copy(tokens_ref, x, local.at[0])
+    load_x.start()
+    load_w = [pltpu.make_async_copy(s, w.at[j, own, :], local.at[1 + j]) for j, s in enumerate(shards)]
+    load_pack = pltpu.make_async_copy(pack_ref, pack.at[core], local.at[5])
+    load_bup = pltpu.make_async_copy(bup_ref, bups_ref.at[core], local.at[6])
+    load_up = pltpu.make_async_copy(up_ref, up, local.at[7])
+    load_down = pltpu.make_async_copy(down_ref, wdown_ref.at[ff_own, :], local.at[8])
+    for load in (load_pack, *load_w, load_bup, load_up, load_down):
+        load.start()
+    zeros[...] = jnp.zeros_like(zeros)
+    gap = TILES * TILE - FF_HALF
+    blanks = [
+        pltpu.make_async_copy(
+            zeros, wdown_ref.at[pl.ds(h * TILES * TILE + FF_HALF, gap), :], local.at[9 + h]
+        )
+        for h in (0, 1)
+    ]
+    for blank in blanks:
+        blank.start()
+
+    bar = pltpu.get_barrier_semaphore()
+    pl.semaphore_signal(bar, inc=1, device_id=(1 - core, at.chip), device_id_type=MESH)
+    pl.semaphore_wait(bar, 1)
+
+    def share(j, source, target):
+        return at.copy_sibling(source, target, sent.at[j], got.at[j])
+
+    give_w = [share(j, s, w.at[j, own, :]) for j, s in enumerate(shards)]
+    give_pack = share(4, pack_ref, pack.at[core])
+    give_bup = share(5, bup_ref, bups_ref.at[core])
+    give_down = share(6, down_ref, wdown_ref.at[ff_own, :])
+    give_up = share(7, up_wide, wup_ref.at[own, :])
+    keep_up = pltpu.make_async_copy(up_wide, wup_ref.at[own, :], local.at[11])
+    give_pack.start()
+    for give in give_w:
+        give.start()
+    give_bup.start()
+    give_down.start()
+
+    load_pack.wait()
+    give_pack.wait()
+    vec[...] = jnp.concatenate([pack[0, :, :HALF], pack[1, :, :HALF]], axis=1)
+    load_x.wait()
+    rows_of = [pl.ds(b * 512, 512) for b in range(2)]
+
+    def first_norm(b, carry):
+        rows = pl.ds(aligned(b * 128, 128), 128)
+        h1[rows, :] = normalise(x[rows, :].astype(f32), vec[0:1, :], vec[1:2, :]).astype(bf16)
+        return carry
+
+    lax.fori_loop(0, 8, first_norm, 0)
+    keep = [pltpu.make_async_copy(h1, h1_ref, local.at[0])]
+    keep[0].start()
+
+    def project(j, target, bias):
+        load_w[j].wait()
+        give_w[j].wait()
+        for rows in rows_of:
+            y = dot(h1[rows, :], w[j], NN)
+            if bias is not None:
+                y = y + vec[bias : bias + 1, :]
+            target[rows, :] = y.astype(bf16)
+
+    project(0, q, 2)
+    project(1, k, None)
+    project(2, v, 3)
+    for j, (s, d) in enumerate(((q, q_ref), (k, k_ref), (v, v_ref))):
+        keep.append(pltpu.make_async_copy(s, d, local.at[12 + j]))
+        keep[-1].start()
+
+    load_up.wait()
+
+    def widen(b, carry):
+        rows = pl.ds(aligned(b * 64, 64), 64)
+        row = up[rows, :]
+        none = jnp.zeros((64, gap), bf16)
+        up_wide[rows, :] = jnp.concatenate([row[:, :FF_HALF], none, row[:, FF_HALF:], none], axis=1)
+        return carry
+
+    lax.fori_loop(0, HALF // 64, widen, 0)
+    keep_up.start()
+    give_up.start()
+
+    def keep_probs(i):
+        slot = lax.rem(i, 2)
+        return pltpu.make_async_copy(probs.at[slot], probs_ref.at[i], psem.at[slot])
+
+    def attention(i, carry):
+        rows = pl.ds(aligned(i * 128, 128), 128)
+        slot = lax.rem(i, 2)
+
+        @pl.when(i >= 2)
+        def _():
+            keep_probs(i - 2).wait()
+
+        qi, ki, vi = q[rows, :], k[rows, :], v[rows, :]
+        mixed = Lanes()
+        held = []
+        for h in range(HEADS):
+            cols = head_window(h)
+            logits = dot(qi[:, cols], only_head(ki[:, cols], h), NT) * SCALE
+            e = jnp.exp(logits - jnp.max(logits, axis=-1, keepdims=True))
+            p = (e / jnp.sum(e, axis=-1, keepdims=True)).astype(bf16)
+            held.append(p)
+            mixed.add(h, dot(p, only_head(vi[:, cols], h), NN))
+        ao[rows, :] = mixed.joined()
+        probs[slot] = jnp.concatenate(held, axis=1)
+        keep_probs(i).start()
+        return carry
+
+    lax.fori_loop(0, 8, attention, 0)
+    keep_ao = pltpu.make_async_copy(ao, ao_ref, local.at[15])
+    keep_ao.start()
+
+    load_w[3].wait()
+    give_w[3].wait()
+    keep_w = pltpu.make_async_copy(w, w_ref, wsem.at[0])
+    keep_w.start()
+    keep_vec = pltpu.make_async_copy(vec, vec_ref, wsem.at[1])
+    keep_vec.start()
+    for rows in rows_of:
+        x2[rows, :] = x[rows, :].astype(f32) + dot(ao[rows, :], w[3], NN) + vec[4:5, :]
+
+    def second_norm(b, carry):
+        rows = pl.ds(aligned(b * 128, 128), 128)
+        h2[rows, :] = normalise(x2[rows, :], vec[5:6, :], vec[6:7, :]).astype(bf16)
+        return carry
+
+    lax.fori_loop(0, 8, second_norm, 0)
+    keep_x2 = pltpu.make_async_copy(x2, x2_ref, wsem.at[2])
+    keep_h2 = pltpu.make_async_copy(h2, h2_ref, wsem.at[3])
+    for copy in (keep_x2, keep_h2):
+        copy.start()
+    for copy in (
+        *keep,
+        keep_probs(6),
+        keep_probs(7),
+        keep_ao,
+        keep_w,
+        keep_vec,
+        load_bup,
+        load_down,
+        *blanks,
+        keep_up,
+        keep_x2,
+        keep_h2,
+    ):
+        copy.wait()
+    for give in (give_bup, give_down, give_up):
+        give.wait()
+
+
+def forward(tokens, wq, wk, wv, wo, up, down, pack, bup):
+    rows = tokens.shape[0]
+    images = rows // PATCHES
+    flat = jax.ShapeDtypeStruct((rows, WIDTH), bf16)
+    return pl.pallas_call(
+        forward_kernel,
+        out_shape=(
+            flat,
+            flat,
+            flat,
+            flat,
+            flat,
+            jax.ShapeDtypeStruct((images, PATCHES, HEADS * PATCHES), bf16),
+            jax.ShapeDtypeStruct((rows, WIDTH), f32),
+            flat,
+            jax.ShapeDtypeStruct((4, WIDTH, WIDTH), bf16),
+            jax.ShapeDtypeStruct((WIDTH, FF_PAD), bf16),
+            jax.ShapeDtypeStruct((FF_PAD, WIDTH), bf16),
+            jax.ShapeDtypeStruct((VECTORS, WIDTH), f32),
+            jax.ShapeDtypeStruct((2, TILES, 1, TILE), f32),
+        ),
+        in_specs=[ANY] * 9,
+        out_specs=[ANY] * 13,
+        scratch_shapes=[pltpu.VMEM((rows, WIDTH), bf16)] * 6
+        + [
+            pltpu.VMEM((2, PATCHES, HEADS * PATCHES), bf16),
+            pltpu.VMEM((rows, WIDTH), f32),
+            pltpu.VMEM((rows, WIDTH), bf16),
+            pltpu.VMEM((4, WIDTH, WIDTH), bf16),
+            pltpu.VMEM((HALF, FF), bf16),
+            pltpu.VMEM((HALF, FF_PAD), bf16),
+            pltpu.VMEM((TILES * TILE - FF_HALF, WIDTH), bf16),
+            pltpu.VMEM((2, VECTORS, LANES), f32),
+            pltpu.VMEM((VECTORS, WIDTH), f32),
+            pltpu.SemaphoreType.DMA((16,)),
+            pltpu.SemaphoreType.DMA((4,)),
+            pltpu.SemaphoreType.DMA((2,)),
+            pltpu.SemaphoreType.DMA((8,)),
+            pltpu.SemaphoreType.DMA((8,)),
+            pltpu.SemaphoreType.DMA((1,)),
+        ],
+        compiler_params=pltpu.CompilerParams(
+            collective_id=3, has_side_effects=True, vmem_limit_bytes=62 * 2**20
+        ),
+        name="forward",
+    )(tokens, wq, wk, wv, wo, up, down, pack, bup)
+
+
+def finish_kernel(g1_ref, g2_ref, g3_ref, d1_ref, d2_ref, dq_ref, dk_ref, dv_ref, do_ref):
+    d1_ref[...] = g1_ref[0].astype(f32)
+    parts = []
+    for h in (0, 1):
+        for i in range(TILES):
+            wide = TILE if i < TILES - 1 else FF_HALF - (TILES - 1) * TILE
+            parts.append(g2_ref[i, :, h * TILE : h * TILE + wide].astype(f32))
+    d2_ref[...] = jnp.concatenate(parts, axis=1)
+    for j, d in enumerate((dq_ref, dk_ref, dv_ref, do_ref)):
+        d[...] = g3_ref[j].astype(f32)
+
+
+def finish(g1, g2, g3):
+    steps = HALF // 32
+    square = jax.ShapeDtypeStruct((HALF, WIDTH), f32)
+    last = TILES - 1
+    return pl.pallas_call(
+        finish_kernel,
+        grid=(steps,),
+        out_shape=(
+            jax.ShapeDtypeStruct((FF_HALF, WIDTH), f32),
+            jax.ShapeDtypeStruct((HALF, FF), f32),
+        )
+        + (square,) * 4,
+        in_specs=[
+            pl.BlockSpec((1, TILE, WIDTH), lambda i: (jnp.minimum(i, last), 0, 0)),
+            pl.BlockSpec((TILES, 32, 2 * TILE), lambda i: (0, i, 0)),
+            pl.BlockSpec((4, 32, WIDTH), lambda i: (0, i, 0)),
+        ],
+        out_specs=[
+            pl.BlockSpec((TILE, WIDTH), lambda i: (jnp.minimum(i, last), 0)),
+            pl.BlockSpec((32, FF), lambda i: (i, 0)),
+        ]
+        + [pl.BlockSpec((32, WIDTH), lambda i: (i, 0))] * 4,
+        compiler_params=pltpu.CompilerParams(vmem_limit_bytes=48 * 2**20),
+        name="finish",
+    )(g1, g2, g3)
 
 
 def fast_shards(
@@ -895,44 +1216,20 @@
     down_weight,
     down_bias,
 ):
+    small = [ln1_gain, ln1_bias, q_bias, v_bias, o_bias, ln2_gain, ln2_bias, down_bias]
+    pack = jnp.pad(jnp.stack(small).astype(f32), ((0, 0), (0, LANES - HALF)))
     gap = TILES * TILE - FF_HALF
-    gain_one, shift_one, wq, bq, wk, wv, bv, wo, bo, gain_two, shift_two, bdown = [
-        gather(v)
-        for v in (
-            ln1_gain,
-            ln1_bias,
-            q_weight,
-            q_bias,
-            k_weight,
-            v_weight,
-            v_bias,
-            o_weight,
-            o_bias,
-            ln2_gain,
-            ln2_bias,
-            down_bias,
-        )
-    ]
-    up_parts = jnp.pad(up_weight.reshape(HALF, 2, FF_HALF), ((0, 0), (0, 0), (0, gap)))
-    wup = gather(up_parts.reshape(HALF, FF_PAD))
-    wdown = gather(jnp.pad(down_weight, ((0, gap), (0, 0))))
-    bup = gather(jnp.pad(up_bias, (0, gap)))
-    bup = bup.reshape(2, TILES, TILE).transpose(1, 0, 2).reshape(TILES, 1, 2 * TILE)
-
+    bup = jnp.pad(up_bias.astype(f32), (0, gap)).reshape(TILES, 1, TILE)
+    normed1, query, key_rows, value_rows, attn_in, probs, residual, normed2, w, wup, wdown, vec, bup = (
+        forward(tokens, q_weight, k_weight, v_weight, o_weight, up_weight, down_weight, pack, bup)
+    )
+    wq, wk, wv, wo = w[0], w[1], w[2], w[3]
     input_f = tokens.astype(f32)
-    gain_one, shift_one = gain_one.astype(f32), shift_one.astype(f32)
-    gain_two, shift_two = gain_two.astype(f32), shift_two.astype(f32)
-    normed1 = layer_norm(input_f, gain_one, shift_one).astype(bf16)
-    query = (jnp.dot(normed1, wq, preferred_element_type=f32) + bq.astype(f32)).astype(bf16)
-    key_rows = jnp.dot(normed1, wk, preferred_element_type=f32).astype(bf16)
-    value_rows = (jnp.dot(normed1, wv, preferred_element_type=f32) + bv.astype(f32)).astype(bf16)
-    mixed, log_total = attend(query, key_rows, value_rows)
-    attn_in = mixed.astype(bf16)
-    residual = input_f + jnp.dot(attn_in, wo, preferred_element_type=f32) + bo.astype(f32)
-    normed2 = layer_norm(residual, gain_two, shift_two).astype(bf16)
+    gain_one, shift_one, gain_two, shift_two = vec[0], vec[1], vec[5], vec[6]
+    log_total = attend(query, key_rows, value_rows)[1]
 
     output, d_normed2, g1, g2, d_bup = feed_forward(
-        normed2, residual, out_grad, wup, wdown, bup, bdown.reshape(1, WIDTH)
+        normed2, residual, out_grad, wup, wdown, bup, vec
     )
 
     _, norm_back_two = jax.vjp(layer_norm, residual, gain_two, shift_two)
@@ -970,21 +1267,18 @@
     mine = lax.dynamic_index_in_dim(pack, lax.axis_index("group"), 0, keepdims=False)
     small = [mine[j * HALF : (j + 1) * HALF] for j in range(8)]
 
-    g1 = g1.reshape(TILES * TILE, WIDTH)[:FF_HALF].astype(f32)
-    g2 = g2.reshape(TILES, HALF, 2, TILE).transpose(1, 2, 0, 3).reshape(HALF, 2, TILES * TILE)
-    g2 = g2[:, :, :FF_HALF].reshape(HALF, FF).astype(f32)
-    g3 = g3.astype(f32)
+    g1, g2, gq, gk, gv, go = finish(g1, g2, g3)
     return (
         output,
         d_input,
         small[0],
         small[1],
-        g3[0],
+        gq,
         small[2],
-        g3[1],
-        g3[2],
+        gk,
+        gv,
         small[3],
-        g3[3],
+        go,
         small[4],
         small[5],
         small[6],

time: 717 us -> 743 us (1.036)
  Pallas kernels: 344 us -> 514 us
  local copies, waits for them, and re-layouts: 159 us -> 82.5 us
  matrix products: 91.9 us -> 59.4 us
  other arithmetic: 50 us -> 32.9 us
  between operations: 15.9 us -> 1.39 us
    pallas_call x0 -> x2, Pallas kernels: none -> 170 us  [the longest x1 152 us: forward(): pl.pallas_call(forward_kernel, out_shape=(flat, flat, flat, flat, flat, j...]
    reshape x6 -> x1, local copies, waits for them, and re-layouts: 32.9 us -> 0.61 us  [fast_shards(): bup = jnp.pad(up_bias.astype(f32), (0, gap)).reshape(TILES, 1, TILE)]
    dot_general x5 -> x0, matrix products: 29.2 us -> none  [the longest x1 7.32 us: fast_shards(): jnp.dot(normed1, wv, preferred_element_type=f32) + bv.astype(f32)]
    convert_element_type x11 -> x0, other arithmetic: 20.1 us -> none  [the longest x1 7.44 us: fast_shards(): g2 = g2[:, :, :FF_HALF].reshape(HALF, FF).astype(f32)]
    unnamed x101 -> x49, local copies, waits for them, and re-layouts: 28.6 us -> 9.69 us
    pad x3 -> x0, local copies, waits for them, and re-layouts: 13.6 us -> none  [the longest x1 8.65 us: fast_shards(): jnp.pad(up_weight.reshape(HALF, 2, FF_HALF), ((0, 0), (0, 0), (0, gap)))]
    reshape x8 -> x7, local copies, waits for them, and re-layouts: 61.4 us -> 57 us  [split_heads(): return rows.reshape(-1, PATCHES, HEADS, rows.shape[-1] // HEADS)]
  transfers between devices with their start and end apart: 6 -> 0, of which waited for: 0 -> 0; matrix products, arithmetic and copies ran while one was open for 17% -> 0% of each run, Pallas kernels for 0% -> 0%
where the time goes in v2:
time: 743 us; the launch traced here: 729 us
  Pallas kernels  514 us (69%)
  local copies, waits for them, and re-layouts  82.5 us (11%)
  matrix products  59.4 us (8%)
  blocking collectives  38.7 us (5%)
  other arithmetic  32.9 us (4%)
    pallas_call x1, Pallas kernels, feed_forward(): pl.pallas_call(ff_kernel, out_shape=(jax.ShapeDtypeStruct((rows, WIDTH),...  220 us
    pallas_call x1, Pallas kernels, forward(): pl.pallas_call(forward_kernel, out_shape=(flat, flat, flat, flat, flat, j...  152 us
    pallas_call x1, Pallas kernels, attention_sum(): pl.pallas_call(attention_sum_kernel, out_shape=jax.ShapeDtypeStruct((2, C...  124 us
    reshape x7, local copies, waits for them, and re-layouts, split_heads(): return rows.reshape(-1, PATCHES, HEADS, rows.shape[-1] // HEADS)  57 us
    psum x1, blocking collectives, fast_shards(): pack = lax.psum(pack, ('group', 'replica')).astype(f32)  38.7 us
    dot_general x4, matrix products, back_rows(): jnp.einsum('rb,ab->ra', grads, weight, preferred_element_type=jnp.float32)  24 us
    pallas_call x1, Pallas kernels, finish(): pl.pallas_call(finish_kernel, grid=(steps,), out_shape=(jax.ShapeDtypeStr...  18.1 us
    dot_general x4, matrix products, outer_rows(): jnp.einsum('ra,rb->ab', left, right, preferred_element_type=jnp.float32)  15.8 us

profile of v2, /device:TPU:0, one launch (start us, length us, event | category | flops | bytes accessed | tf_op | source)
XLA Modules:
  0.0 728.7 jit_solution(4082145139829684670)
XLA Ops:
  0.7 0.7 stack.27
  6.8 0.7 pad_convert_fusion.1
  8.1 151.9 %forward.1 = (bf16[1024,1152]{1,0:T(8,128)(2,1)}, bf16[1024,1152]{1,0:T(8,128)(2,1)}, bf16[1024,1152]{1,0:T(8,128)(2,1)}, bf16[1024,1152]{1,0:T(8,128)(2,1)}, bf...) custom-call(bf16[1024,1152]{1,0:T(8,128)(2,1)} %tokens_ref.1, ...), custom_call_target="tpu_custom_call" | custom-call | tf_op jit(solution)/shard_map/forward/pallas_call | solution.py:1117
  160.0 220.0 %feed_forward.1 = (bf16[1024,1152]{1,0:T(8,128)(2,1)}, f32[1024,1152]{1,0:T(8,128)}, bf16[17,128,1152]{2,1,0:T(8,128)(2,1)}, bf16[17,576,256]{2,1,0:T(8,128)(2,1)}, f32[17,1,256]{2,1,0:T(1,128)}) custom-call(bf16[1024,1152]{1,0:T(8,128)(2,1)} %get-tuple-element.40.h2_ref, f32[1024,1152]{1,0:T(8,128)} %get-tuple-element.41.x2_ref, bf16[1024,1152]{1,0:T(8,128)(2,1)} %og_ref.1, ...), custom_call_target="tpu_custom_call" | custom-call | tf_op jit(solution)/shard_map/feed_forward/pallas_call | solution.py:759
  380.1 2.6 reduce_sum.156
  382.7 3.1 multiply_reduce_fusion.4
  385.8 1.6 slice_reduce_fusion.1
  387.4 3.7 multiply_reduce_fusion.2
  391.2 1.9 fusion.49
  393.5 1.2 fusion.47
  395.2 1.4 copy-done.10
  396.6 6.6 convolution_convert_fusion.4
  403.2 9.6 %reshape.237 = bf16[8,128,16,72]{3,2,1,0:T(8,128)(2,1)} reshape(bf16[1024,1152]{1,0:T(8,128)(2,1)} %convolution_convert_fusion.4) | data formatting | bytes 4718592 | tf_op jit(solution)/shard_map/reshape | solution.py:25
  412.8 6.2 copy.54
  418.9 9.6 %reshape.236 = bf16[8,128,16,72]{3,2,1,0:T(8,128)(2,1)} reshape(bf16[1024,1152]{1,0:T(8,128)(2,1)} %get-tuple-element.49) | data formatting | bytes 4718592 | tf_op jit(solution)/shard_map/reshape | solution.py:25
  428.5 6.2 copy.50
  434.7 9.6 %reshape.235 = bf16[8,128,16,72]{3,2,1,0:T(8,128)(2,1)} reshape(bf16[1024,1152]{1,0:T(8,128)(2,1)} %get-tuple-element.48) | data formatting | bytes 4718592 | tf_op jit(solution)/shard_map/reshape | solution.py:25
  444.2 6.3 copy.56
  450.6 4.0 multiply_reduce_fusion.1
  454.6 2.4 exponential_reduce_fusion
  457.0 1.0 copy-done.9
  458.0 3.1 fusion.51
  461.1 2.9 copy.64
  464.0 9.6 %reshape.234 = bf16[8,128,16,72]{3,2,1,0:T(8,128)(2,1)} reshape(bf16[1024,1152]{1,0:T(8,128)(2,1)} %get-tuple-element.51) | data formatting | bytes 4718592 | tf_op jit(solution)/shard_map/reshape | solution.py:25
  473.6 7.8 %multiply_reduce_fusion = (f32[8,16,128]{2,1,0:T(8,128)S(1)}, f32[8,16,128,128]{2,3,1,0:T(8,128)S(1)}) fusion(f32[8,16,128,128]{2,3,1,0:T(8,128)} %copy-done.1, f32[8,16,128]{2,1,0:T(8,128)S(1)} %log_add_fusion, bf16[8,128,16,72]{1,3,2,0:T(8,128)(2,1)} %copy.54, bf16[8,128,16,72]{3,2,1,0:T(8,128)(2,1)} %reshape.234), kind=kOutput, calls=%fused_computation.2 | convolution fusion | flops 310362112 | bytes 21626880 | tf_op jit(solution)/shard_map/isha,itha->ihst/dot_general | solution.py:55
  481.4 5.4 multiply_convert_fusion
  486.9 1.7 fusion.50
  488.6 1.5 copy.58
  490.1 1.4 copy-done.14
  491.5 5.4 fusion.19
  497.0 3.0 fusion.27
  500.0 1.5 copy.61
  501.6 1.4 copy-done.16
  503.0 5.9 fusion.17
  508.9 6.1 fusion.46
  515.0 2.4 fusion.8
  517.5 3.3 add_convert_fusion
  521.7 38.7 %psum.7 = bf16[2,6760]{1,0:T(2,128)(2,1)S(1)} all-reduce(bf16[2,6760]{1,0:T(2,128)(2,1)S(1)} %concatenate.7), channel_id=1, replica_groups=mesh['group'=2,'replica'=16] {'group','replica'}, use_global_device_ids=true, to_apply=%region_19.20 | all-reduce | flops 13520 | bytes 54080 | tf_op jit(solution)/shard_map/psum | solution.py:1266
  560.4 0.7 slice_reduce_fusion.3
  561.1 5.8 convolution_convert_fusion
  566.9 3.3 convolution_convert_fusion.1
  570.2 3.3 convolution_convert_fusion.2
  573.5 3.5 convolution_convert_fusion.3
  577.0 5.1 pad_maximum_fusion
  582.1 123.8 %attention_sum.1 = bf16[2,9,128,1152]{3,2,1,0:T(8,128)(2,1)} custom-call(bf16[2,2,9,128,1152]{4,3,2,1,0:T(8,128)(2,1)} %bitcast.83), custom_call_target="tpu_custom_call" | custom-call | tf_op jit(solution)/shard_map/attention_sum/pallas_call | solution.py:854
  705.9 2.4 copy-done
  708.3 18.1 %finish.1 = (f32[2152,1152]{1,0:T(8,128)}, f32[576,4304]{1,0:T(8,128)}, f32[576,1152]{1,0:T(8,128)}, f32[576,1152]{1,0:T(8,128)}, f32[576,1152]{1,0:T(8,128)}, /*index=5*/f32[576,1152]{1,0:T(8,128)}) custom-call(bf16[17,128,1152]{2,1,0:T(8,128)(2,1)S(1)} %copy-done, bf16[17,576,256]{2,1,0:T(8,128)(2,1)} %get-tuple-element.54.g2_ref, ...), custom_call_target="tpu_custom_call" | custom-call | tf_op jit(solution)/shard_map/finish/pallas_call | solution.py:1177
  727.1 1.4 copy.114
  (76 shorter events, 8.8 us)
Async XLA Ops:
  382.7 4.7 copy-start.2
  382.7 8.4 %slice-start.2 = ((s8[4718592]{0:T(1024)(128)(4,1)}), s8[4194304]{0:T(1024)(128)(4,1)S(1)}, s32[]{:S(2)}) async-start(s8[4718592]{0:T(1024)(128)(4,1)} %bitcast.85), calls=%async_computation.2 | async-start | bytes 8388608
  387.4 3.7 slice-start.3
  391.1 1.9 copy-start.4
  391.1 2.4 copy-start.5
  393.0 2.2 copy-start.3
  395.2 1.4 copy-start.10
  454.5 6.5 copy-start.1
  454.6 3.4 copy-start.9
  481.4 5.4 copy-start.8
  490.1 1.4 copy-start.14
  491.5 5.5 copy-start.7
  501.6 1.4 copy-start.16
  503.0 5.9 copy-start.12
  503.0 14.5 %slice-start = ((s8[4718592]{0:T(1024)(128)(4,1)}), s8[4194304]{0:T(1024)(128)(4,1)S(1)}, s32[]{:S(2)}) async-start(s8[4718592]{0:T(1024)(128)(4,1)} %bitcast.81), calls=%async_computation | async-start | bytes 8388608
  508.9 8.6 %slice-start.1 = ((s8[4718592]{0:T(1024)(128)(4,1)}), s8[524288]{0:T(1024)(128)(4,1)S(1)}, s32[]{:S(2)}) async-start(s8[4718592]{0:T(1024)(128)(4,1)} %bitcast.81), calls=%async_computation.1 | async-start | bytes 1048576
  515.0 2.5 copy-start.6
  517.5 4.0 copy-start.18
  561.1 5.8 copy-start.13
  561.1 5.8 copy-start.19
  566.9 3.3 copy-start.17
  570.2 3.3 copy-start.15
  705.9 2.4 copy-start
  708.3 18.7 %copy-start.11 = (bf16[1024,1152]{1,0:T(8,128)(2,1)S(1)}, bf16[1024,1152]{1,0:T(8,128)(2,1)}, u32[]{:S(2)}) copy-start(bf16[1024,1152]{1,0:T(8,128)(2,1)} %get-tuple-element.116) | copy-start | bytes 7077892
